TPU v7x, 512 devices: a whole 4x8x8 slice. The times are simulated.
512 devices in a mesh: tm: 64 (over y, z), plane: 8 (over x, core).
Axes of the slice: x: 4, y: 8, z: 8, core: 2. Of those that a mesh axis runs over, the one named last changes fastest.
Arguments:
- frames: bfloat16 [64, 16, 128, 1024], P('tm', 'plane'), may hold values from -6 to 6
- offsets: int32 [64, 16, 2], P('tm', 'plane'), may hold values from -64 to 64
- assign: int32 [64, 16, 1, 8, 1], P('tm', 'plane'), may hold values from 0 to 7; in each aligned block of 16 rows (0 to 15, 16 to 31, ..., all dimensions but the last counted through in order) at most 4 rows name the same one
- residual: int32 [64, 16, 1, 8, 2], P('tm', 'plane'), may hold values from -8 to 8
- template: bfloat16 [16, 128, 1024], P(None, None, 'plane'), may hold values from -6 to 6
Outputs:
- new_template: bfloat16 [16, 128, 1024], P(None, None, 'plane')
- scores: float32 [2, 64, 16, 1, 8], P(None, 'tm', 'plane')
Inputs may be any that keep to these rules, and one draw needn't show every extreme that they name: `assign`: in each aligned block of 16 rows (the patches of one volume and one plane group), no column is named more than 4 times; one column is named exactly 4 times in some block.
All inputs are finite; a program needn't handle non-finite values.
Results may differ from a plain program's by a relative error of at most 0.004.
Values may be sent and summed in bfloat16 or wider, within the bound.
No kernel may reach another device: no remote copies, remote signals or barrier semaphores. Data moves between devices by JAX's collectives and lax.ppermute only.
A program may use at most 64 MiB of HBM per device.

v0:
```python
import math

import jax
import jax.numpy as jnp
from jax import lax
from jax.sharding import PartitionSpec as P

ROUNDS = 2


highest = lax.Precision.HIGHEST


def dft_tables(length):
    indices = jnp.arange(length, dtype=jnp.int32)
    phases = (indices[:, None] * indices[None, :] % length).astype(jnp.float32) * (
        2.0 * math.pi / length
    )
    return (jnp.cos(phases).astype(jnp.bfloat16), jnp.sin(phases).astype(jnp.bfloat16))


def cyclic(source, amount, which_axis):
    length = source.shape[which_axis]
    doubled = jnp.concatenate([source, source], which_axis)
    return lax.dynamic_slice_in_dim(
        doubled, (amount % length).astype(jnp.int32), length, which_axis
    )


def shift_plane(frame_img, plane_off):
    return cyclic(cyclic(frame_img, plane_off[0], 0), plane_off[1], 1)


def to_tiles(tile_batch, patch_size):
    plane_count, tall, broad = tile_batch.shape
    shaped = tile_batch.reshape(
        plane_count, tall // patch_size, patch_size, broad // patch_size, patch_size
    )
    return shaped.transpose(0, 1, 3, 2, 4)


def spectrum(tile_batch, cos_t, sin_t):
    first_re = jnp.einsum(
        "nyx,xk->nyk", tile_batch, cos_t, preferred_element_type=jnp.float32
    ).astype(jnp.bfloat16)
    first_im = (
        -jnp.einsum("nyx,xk->nyk", tile_batch, sin_t, preferred_element_type=jnp.float32)
    ).astype(jnp.bfloat16)
    spec_re = jnp.einsum(
        "uy,nyk->nuk", cos_t, first_re, preferred_element_type=jnp.float32
    ) + jnp.einsum("uy,nyk->nuk", sin_t, first_im, preferred_element_type=jnp.float32)
    spec_im = jnp.einsum(
        "uy,nyk->nuk", cos_t, first_im, preferred_element_type=jnp.float32
    ) - jnp.einsum("uy,nyk->nuk", sin_t, first_re, preferred_element_type=jnp.float32)
    return (spec_re, spec_im)


def assess(patches, temp_re, temp_im, shift_rows, shift_cols, live_mask, cos_t, sin_t):
    patch_size = patches.shape[1]
    patch_re, patch_im = spectrum(patches, cos_t, sin_t)
    cross_re = patch_re * temp_re + patch_im * temp_im
    cross_im = patch_im * temp_re - patch_re * temp_im
    modulus = jnp.sqrt(cross_re * cross_re + cross_im * cross_im)
    levels = jnp.mean(modulus, axis=(1, 2), keepdims=True)
    divisor = modulus + 0.1 * levels + 1e-06
    norm_re = (cross_re / divisor).astype(jnp.bfloat16)
    norm_im = (cross_im / divisor).astype(jnp.bfloat16)
    row_a = (shift_rows % patch_size).astype(jnp.int32)
    row_b = (shift_cols % patch_size).astype(jnp.int32)
    cos_a = cos_t[row_a].astype(jnp.float32)
    sin_a = sin_t[row_a].astype(jnp.float32)
    cos_b = cos_t[row_b]
    sin_b = sin_t[row_b]
    re_cos = jnp.einsum("nuv,nv->nu", norm_re, cos_b, preferred_element_type=jnp.float32)
    re_sin = jnp.einsum("nuv,nv->nu", norm_re, sin_b, preferred_element_type=jnp.float32)
    im_cos = jnp.einsum("nuv,nv->nu", norm_im, cos_b, preferred_element_type=jnp.float32)
    im_sin = jnp.einsum("nuv,nv->nu", norm_im, sin_b, preferred_element_type=jnp.float32)
    scores = (
        jnp.sum(cos_a * re_cos, 1)
        - jnp.sum(sin_a * re_sin, 1)
        - jnp.sum(sin_a * im_cos, 1)
        - jnp.sum(cos_a * im_sin, 1)
    ) / patch_size
    weights = (0.5 + jax.nn.sigmoid(scores)) * live_mask
    registered = jax.vmap(
        lambda single, shift_down, shift_across: cyclic(
            cyclic(single, shift_down, 0), shift_across, 1
        )
    )(patches, shift_rows, shift_cols)
    contrib = registered.astype(jnp.float32) * weights[:, None, None]
    return (contrib, weights, scores)


def renew(old_rows_all, tile_sums, weight_sums, patch_size):
    totals, weight_all = lax.psum((tile_sums, weight_sums), "tm")
    return (
        (old_rows_all.astype(jnp.float32) + totals)
        / (1.0 + jnp.repeat(weight_all, patch_size))[:, None]
    ).astype(jnp.bfloat16)


def local(frames, offsets, assign, residual, template):
    patch_size = template.shape[2]
    planes_all = template.shape[0]
    grid_rows = template.shape[1] // patch_size
    owners = lax.axis_size("plane")
    plane_dev = frames.shape[1]
    patch_count = plane_dev * grid_rows * owners
    capacity = 2 * patch_count // owners
    plane_group = lax.axis_index("plane")
    cos_t, sin_t = dft_tables(patch_size)
    shifted = jax.vmap(shift_plane)(frames[0], offsets[0])
    patches = to_tiles(shifted, patch_size).reshape(patch_count, patch_size, patch_size)
    owner_col = assign.reshape(patch_count)
    shift_rows = residual[0, :, :, :, 0].reshape(patch_count)
    shift_cols = residual[0, :, :, :, 1].reshape(patch_count)
    counter = jnp.arange(patch_count, dtype=jnp.int32)
    plane_local = counter // (grid_rows * owners)
    row_local = counter // owners % grid_rows
    score_list = []
    column_hit = (owner_col[:, None] == jnp.arange(owners, dtype=jnp.int32)[None, :]).astype(
        jnp.int32
    )
    position = jnp.sum(jnp.cumsum(column_hit, 0) * column_hit, 1) - 1
    slot_index = owner_col * capacity + position
    slot_count = owners * capacity
    placing = slot_index[:, None] == jnp.arange(slot_count, dtype=jnp.int32)[None, :]
    outgoing = jnp.einsum(
        "rs,rxy->sxy", placing.astype(jnp.bfloat16), patches, preferred_element_type=jnp.float32
    ).astype(jnp.bfloat16)
    outgoing = outgoing.reshape(owners, capacity, patch_size, patch_size)
    details = jnp.stack(
        [
            plane_group * plane_dev + plane_local,
            row_local,
            shift_rows,
            shift_cols,
            jnp.ones_like(shift_rows),
        ],
        1,
    )
    outgoing_info = jnp.sum(placing.astype(jnp.int32)[:, :, None] * details[:, None, :], 0).reshape(
        owners, capacity, 5
    )
    current = template
    for round_index in range(ROUNDS):
        tile_stack = current
        temp_re, temp_im = spectrum(tile_stack, cos_t, sin_t)
        arrived = lax.all_to_all(outgoing, "plane", split_axis=0, concat_axis=0, tiled=True)
        arrived_info = lax.all_to_all(
            outgoing_info, "plane", split_axis=0, concat_axis=0, tiled=True
        )
        senders = arrived.shape[0]
        held_slots = arrived.shape[1]
        flat_info = arrived_info.reshape(senders * held_slots, 5)
        target = flat_info[:, 0] * grid_rows + flat_info[:, 1]
        contrib, weights, scores = assess(
            arrived.reshape(senders * held_slots, patch_size, patch_size),
            temp_re[target],
            temp_im[target],
            flat_info[:, 2],
            flat_info[:, 3],
            flat_info[:, 4].astype(jnp.float32),
            cos_t,
            sin_t,
        )
        contrib, weights, scores, target = (
            contrib.reshape(senders, held_slots, patch_size, patch_size),
            weights.reshape(senders, held_slots),
            scores.reshape(senders, held_slots),
            target.reshape(senders, held_slots),
        )
        returned = lax.all_to_all(scores, "plane", split_axis=0, concat_axis=0, tiled=True)
        score_rows = jnp.sum(placing.astype(jnp.float32) * returned.reshape(1, slot_count), 1)
        score_list.append(score_rows.reshape(plane_dev, grid_rows, owners))
        onehot = (
            target.reshape(slot_count)[:, None]
            == jnp.arange(planes_all * grid_rows, dtype=jnp.int32)[None, :]
        ).astype(jnp.float32)
        tile_sums = jnp.einsum(
            "st,sxy->txy",
            onehot,
            contrib.reshape(slot_count, patch_size, patch_size),
            precision=highest,
        )
        weight_sums = jnp.dot(weights.reshape(slot_count), onehot, precision=highest)
        renewed = renew(
            current.reshape(planes_all * grid_rows * patch_size, patch_size),
            tile_sums.reshape(planes_all * grid_rows * patch_size, patch_size),
            weight_sums,
            patch_size,
        )
        current = renewed.reshape(planes_all, grid_rows * patch_size, patch_size)
    return (current, jnp.stack(score_list)[:, None])


def solution(mesh):
    return jax.shard_map(
        local,
        mesh=mesh,
        in_specs=(
            P("tm", "plane", None, None),
            P("tm", "plane", None),
            P("tm", "plane", None, None, None),
            P("tm", "plane", None, None, None),
            P(None, None, "plane"),
        ),
        out_specs=(P(None, None, "plane"), P(None, "tm", "plane", None, None)),
        check_vma=False,
    )
```

profile of v0, /device:TPU:1, one launch (start us, length us, event | category | flops | bytes accessed | tf_op | source)
XLA Modules:
  0.0 452.1 jit_solution(6582208753083625256)
XLA Ops:
  11.3 10.1 %all-to-all-start = ((s32[8,4,5]{2,1,0:T(4,128)}), s32[8,4,5]{2,1,0:T(4,128)S(1)}, u32[]{:S(2)}, u32[]{:S(2)}) async-start(s32[8,4,5]{2,1,0:T(4,128)} %bitcast.1), calls=%async_computation | async-start | bytes 32768 | tf_op jit(solution)/shard_map/all_to_all | solution.py:150
  25.2 3.8 while.2
  29.2 3.9 while.3
  37.6 4.8 %all-to-all-start.1 = ((bf16[8,4,128,128]{3,1,2,0:T(4,128)(2,1)}), bf16[8,4,128,128]{3,1,2,0:T(4,128)(2,1)S(1)}, u32[]{:S(2)}, u32[]{:S(2)}) async-start(bf16[8,4,128,128]{3,1,2,0:T(4,128)(2,1)} %copy.67), calls=%async_computation.1 | async-start | bytes 2097152 | tf_op jit(solution)/shard_map/all_to_all | solution.py:149
  45.3 2.0 gather_fusion.2
  49.3 8.0 %all-to-all-done.1 = bf16[8,4,128,128]{3,1,2,0:T(4,128)(2,1)S(1)} async-done(((bf16[8,4,128,128]{3,1,2,0:T(4,128)(2,1)}), bf16[8,4,128,128]{3,1,2,0:T(4,128)(2,1)S(1)}, u32[]{:S(2)}, u32[]{:S(2)}) %all-to-all-start.1) | async-done | bytes 1048608 | tf_op jit(solution)/shard_map/all_to_all | solution.py:149
  62.8 3.1 fusion.12
  70.0 4.9 %gather_fusion.8 = bf16[32,128,128]{2,0,1:T(8,128)(2,1)S(1)} fusion(bf16[32,256,128]{2,0,1:T(8,128)(2,1)S(1)} %copy.69, s32[32]{0:T(128)S(1)} %fusion.101), kind=kCustom, calls=%fused_computation.8 | custom fusion | bytes 2097536 | tf_op jit(solution)/shard_map/vmap()/gather | solution.py:25
  76.5 4.3 copy.70
  80.8 4.7 %gather_fusion.9 = bf16[32,128,128]{1,0,2:T(8,128)(2,1)S(1)} fusion(bf16[32,128,256]{1,0,2:T(8,128)(2,1)S(1)} %copy.70, s32[32]{0:T(128)S(1)} %fusion.100), kind=kCustom, calls=%fused_computation.9 | custom fusion | bytes 2097536 | tf_op jit(solution)/shard_map/vmap()/gather | solution.py:25
  87.5 2.7 copy.75
  92.5 118.3 %psum.29 = f32[16]{0:T(128)S(1)} all-reduce(f32[16]{0:T(128)S(1)} %convolution_bitcast_fusion.1), channel_id=1, replica_groups=mesh['tm'=64,'plane'=8] {'tm'}, use_global_device_ids=true, to_apply=%region_9.10 | all-reduce | flops 16 | bytes 128 | tf_op jit(solution)/shard_map/psum | solution.py:95
  210.9 37.4 %all-reduce.7.cloned.1.call-done = f32[2048,128]{1,0:T(8,128)} async-done(((f32[2048,128]{1,0:T(8,128)}), f32[2048,128]{1,0:T(8,128)}) %all-reduce.7.cloned.1.call-update) | async-done | bytes 1048592 | tf_op jit(solution)/shard_map/psum | solution.py:95
  253.7 2.0 gather_fusion.7
  255.7 2.8 fusion.5
  258.5 3.4 gather_fusion.6
  261.9 4.3 fusion.13
  269.6 2.3 copy.81
  271.9 2.4 fusion.57
  275.8 13.4 %all_to_all.24 = f32[8,1,4]{2,1,0:T(1,128)S(1)} all-to-all(f32[8,1,4]{2,1,0:T(1,128)S(1)} %bitcast.238), channel_id=1, replica_groups=mesh['tm'=64,'plane'=8] {'plane'}, dimensions={0} | all-to-all | bytes 256 | tf_op jit(solution)/shard_map/all_to_all | solution.py:173
  290.6 113.6 %psum.31 = f32[16]{0:T(128)S(1)} all-reduce(f32[16]{0:T(128)S(1)} %convolution_bitcast_fusion), channel_id=1, replica_groups=mesh['tm'=64,'plane'=8] {'tm'}, use_global_device_ids=true, to_apply=%region_16.17 | all-reduce | flops 16 | bytes 128 | tf_op jit(solution)/shard_map/psum | solution.py:95
  404.9 31.6 %all-to-all-start.3 = ((f32[8,1,4]{2,1,0:T(1,128)}), f32[8,1,4]{2,1,0:T(1,128)S(1)}, u32[]{:S(2)}, u32[]{:S(2)}) async-start(f32[8,1,4]{2,1,0:T(1,128)} %bitcast.57), calls=%async_computation.3 | async-start | bytes 8192 | tf_op jit(solution)/shard_map/all_to_all | solution.py:173
  436.6 4.5 %all-to-all-done.3 = f32[8,1,4]{2,1,0:T(1,128)S(1)} async-done(((f32[8,1,4]{2,1,0:T(1,128)}), f32[8,1,4]{2,1,0:T(1,128)S(1)}, u32[]{:S(2)}, u32[]{:S(2)}) %all-to-all-start.3) | async-done | bytes 160 | tf_op jit(solution)/shard_map/all_to_all | solution.py:173
  442.9 2.4 divide_convert_fusion.4
  (144 shorter events, 54.3 us)
Async XLA Ops:
  7.2 17.7 %copy-start.7 = (bf16[1,2,128,1024]{3,2,1,0:T(8,128)(2,1)S(1)}, bf16[1,2,128,1024]{3,2,1,0:T(8,128)(2,1)}, u32[]{:S(2)}) copy-start(bf16[1,2,128,1024]{3,2,1,0:T(8,128)(2,1)} %param.5) | copy-start | bytes 1572868
  7.2 17.8 %copy-start.8 = (s32[1,2,2]{2,1,0:T(2,128)S(1)}, s32[1,2,2]{2,1,0:T(2,128)}, u32[]{:S(2)}) copy-start(s32[1,2,2]{2,1,0:T(2,128)} %param.6) | copy-start | bytes 52
  11.3 26.3 %all-to-all-start = ((s32[8,4,5]{2,1,0:T(4,128)}), s32[8,4,5]{2,1,0:T(4,128)S(1)}, u32[]{:S(2)}, u32[]{:S(2)}) async-start(s32[8,4,5]{2,1,0:T(4,128)} %bitcast.1), calls=%async_computation | async-start | bytes 32768 | tf_op jit(solution)/shard_map/all_to_all | solution.py:150
  37.6 19.8 %all-to-all-start.1 = ((bf16[8,4,128,128]{3,1,2,0:T(4,128)(2,1)}), bf16[8,4,128,128]{3,1,2,0:T(4,128)(2,1)S(1)}, u32[]{:S(2)}, u32[]{:S(2)}) async-start(bf16[8,4,128,128]{3,1,2,0:T(4,128)(2,1)} %copy.67), calls=%async_computation.1 | async-start | bytes 2097152 | tf_op jit(solution)/shard_map/all_to_all | solution.py:149
  42.4 205.9 %all-reduce.7.cloned.1.call-start = ((), (), s32[]{:S(2)}) async-start(), calls=%async_computation.4 | async-start | bytes 2097152 | tf_op jit(solution)/shard_map/psum | solution.py:95
  60.5 1.6 copy-start.2
  60.5 2.2 copy-start.3
  62.8 3.1 copy-start
  91.0 157.3 %copy-start.6 = (bf16[16,128,128]{2,1,0:T(8,128)(2,1)S(1)}, bf16[16,128,128]{2,1,0:T(8,128)(2,1)}, u32[]{:S(2)}) copy-start(bf16[16,128,128]{2,1,0:T(8,128)(2,1)} %param.9) | copy-start | bytes 1572868
  92.4 350.5 %all-reduce.9.cloned.1.call-start = ((), (), s32[]{:S(2)}) async-start(), calls=%async_computation.5 | async-start | bytes 2097152 | tf_op jit(solution)/shard_map/psum | solution.py:95
  249.9 3.2 copy-start.4
  258.5 3.4 copy-start.1
  274.3 168.6 %copy-start.5 = (bf16[2048,128]{1,0:T(8,128)(2,1)S(1)}, bf16[2048,128]{1,0:T(8,128)(2,1)}, u32[]{:S(2)}) copy-start(bf16[2048,128]{1,0:T(8,128)(2,1)} %copy-done.4) | copy-start | bytes 1572868
  404.9 36.3 %all-to-all-start.3 = ((f32[8,1,4]{2,1,0:T(1,128)}), f32[8,1,4]{2,1,0:T(1,128)S(1)}, u32[]{:S(2)}, u32[]{:S(2)}) async-start(f32[8,1,4]{2,1,0:T(1,128)} %bitcast.57), calls=%async_computation.3 | async-start | bytes 8192 | tf_op jit(solution)/shard_map/all_to_all | solution.py:173
Sparse Core Ops, SparseCore 0:
  92.5 155.7 all-reduce.6
  275.8 157.7 all-reduce.8
where the time goes:
time: 453 us; the launch traced here: 452 us
  blocking collectives  245 us (54%)
  local copies, waits for them, and re-layouts  50.1 us (11%)
  waiting for transfers between devices  50 us (11%)
  starting transfers between devices  46.6 us (10%)
  matrix products  25.4 us (6%)
  other arithmetic  20 us (4%)
  between operations  14.5 us (3%)
    psum x2, blocking collectives, renew(): totals, weight_all = lax.psum((tile_sums, weight_sums), 'tm')  232 us
    psum x2, waiting for transfers between devices, renew(): totals, weight_all = lax.psum((tile_sums, weight_sums), 'tm')  37.4 us
    all_to_all x1, starting transfers between devices, local(): lax.all_to_all(scores, 'plane', split_axis=0, concat_axis=0, tiled=True)  31.6 us
    all_to_all x1, blocking collectives, local(): lax.all_to_all(scores, 'plane', split_axis=0, concat_axis=0, tiled=True)  13.4 us
    all_to_all x1, starting transfers between devices, local(): lax.all_to_all(outgoing_info, 'plane', split_axis=0, concat_axis=0, tiled...  10.1 us
    gather x2, local copies, waits for them, and re-layouts, cyclic(): lax.dynamic_slice_in_dim(doubled, (amount % length).astype(jnp.int32), le...  9.64 us
  transfers between devices with their start and end apart: 5, of which 3 were waited for; matrix products, arithmetic and copies ran while one was open for 6% of the time, Pallas kernels for 0%

commit v1 on v0

v1 whole, which is shorter than its diff:
```python
import functools

import jax
import jax.numpy as jnp
import numpy as np
from jax import lax
from jax.experimental import pallas as pl
from jax.experimental.pallas import tpu as pltpu
from jax.sharding import PartitionSpec as P

N = 128
COLS = 8
PD = 2
K = PD * COLS
TM = 64
SL = TM // PD
RR = N // SL
W = RR * N
F32, BF16 = jnp.float32, jnp.bfloat16


def tables():
    j = np.arange(N, dtype=np.int32)
    phase = (j[:, None] * j[None, :] % N).astype(np.float32) * np.float32(2.0 * np.pi / N)
    cos = np.cos(phase).astype(BF16)
    sin = np.sin(phase).astype(BF16)
    right = np.concatenate([cos, -sin], 1)
    left = np.concatenate(
        [np.concatenate([cos, sin], 1), np.concatenate([-sin, cos], 1)], 0
    )
    rows = np.concatenate([cos, sin], 1).astype(np.float32)
    return right, left, rows


def transform_pair(pair, right, left):
    first = jnp.dot(pair, right, preferred_element_type=F32).astype(BF16)
    inner = jnp.concatenate(
        [
            jnp.concatenate([first[:N, :N], first[N:, :N]], 1),
            jnp.concatenate([first[:N, N:], first[N:, N:]], 1),
        ],
        0,
    )
    return jnp.dot(left, inner, preferred_element_type=F32)


def prep_kernel(off, res, frames, right, left, spec, reg_out, shifted, regs):
    for p in range(PD):
        plane = frames[p].astype(F32)
        plane = pltpu.roll(plane, (-off[p, 0]) & (N - 1), 0)
        plane = pltpu.roll(plane, (-off[p, 1]) & (COLS * N - 1), 1)
        shifted[p] = plane
    for p in range(PD):
        for c in range(0, COLS, 2):
            k = p * COLS + c
            one = shifted[p, :, c * N : (c + 1) * N]
            two = shifted[p, :, (c + 1) * N : (c + 2) * N]
            pair = jnp.concatenate([one, two], 0).astype(BF16)
            both = transform_pair(pair, right[...], left[...])
            spec[k] = both[:, :N]
            spec[k + 1] = both[:, N:]
            for d, patch in ((0, one), (1, two)):
                moved = pltpu.roll(patch, (-res[k + d, 0]) & (N - 1), 0)
                regs[p, c + d] = pltpu.roll(moved, (-res[k + d, 1]) & (N - 1), 1)
        for r in range(RR):
            block = regs[p, :, r * SL : (r + 1) * SL, :]
            block = jnp.transpose(block, (1, 0, 2))
            reg_out[p * SL : (p + 1) * SL, :, r * N : (r + 1) * N] = block.astype(BF16)


def score_patches(asg, res, rows, spec, tspec, srow):
    def one(k, carry):
        tile = (k // COLS) * COLS + asg[k]
        p_re, p_im = spec[k, :N, :], spec[k, N:, :]
        t_re, t_im = tspec[tile, :N, :], tspec[tile, N:, :]
        c_re = p_re * t_re + p_im * t_im
        c_im = p_im * t_re - p_re * t_im
        modulus = jnp.sqrt(c_re * c_re + c_im * c_im)
        level = jnp.sum(jnp.sum(modulus, 0, keepdims=True), 1, keepdims=True) * (1.0 / (N * N))
        scale = 1.0 / (modulus + 0.1 * level + 1e-06)
        n_re = (c_re * scale).astype(BF16)
        n_im = (c_im * scale).astype(BF16)
        row_a = rows[pl.ds(res[k, 0] & (N - 1), 1), :]
        row_b = rows[pl.ds(res[k, 1] & (N - 1), 1), :]
        lhs = jnp.concatenate([row_a[:, :N], row_a[:, N:]], 0).astype(BF16)
        s_re = jnp.dot(lhs, n_re, preferred_element_type=F32)
        s_im = jnp.dot(lhs, n_im, preferred_element_type=F32)
        along = row_b[:, :N] * (s_re[0:1] - s_im[1:2]) - row_b[:, N:] * (s_re[1:2] + s_im[0:1])
        srow[pl.ds(k, 1), :] = along
        return carry

    lax.fori_loop(0, K, one, 0, unroll=2)
    return jnp.sum(srow[...], 1, keepdims=True) * (1.0 / N)


def pieces(value):
    high = value.astype(BF16).astype(F32)
    rest = value - high
    mid = rest.astype(BF16).astype(F32)
    return high, mid, rest - mid


def first_kernel(ids, asg, res, asg_col, temp, spec, reg_in, right, left, rows, msg, score_out, slab, tspec, srow, wide):
    for c in range(COLS):
        both = transform_pair(temp[c], right[...], left[...])
        tspec[c] = both[:, :N]
        tspec[COLS + c] = both[:, N:]
    for c in range(COLS):
        wide[...] = temp[c].astype(F32)
        for r in range(RR):
            slab[c : c + 1, r * N : (r + 1) * N] = wide[pl.ds(ids[0] * N + r * SL + ids[1], 1), :]
    score = score_patches(asg, res, rows, spec, tspec, srow)
    weight = 0.5 + 1.0 / (1.0 + jnp.exp(-score))
    high, mid, low = pieces(weight)
    lane = lax.broadcasted_iota(jnp.int32, (K, N), 1)
    col = asg_col[...]
    meta = jnp.where(lane == 32, 1.0, 0.0)
    meta = jnp.where(lane == col, high, meta)
    meta = jnp.where(lane == col + 8, mid, meta)
    meta = jnp.where(lane == col + 16, low, meta).astype(BF16)
    msg[:, :, :W] = reg_in[...]
    for p in range(PD):
        msg[p * SL : (p + 1) * SL, :, W:] = jnp.broadcast_to(
            meta[p * COLS : (p + 1) * COLS][None], (SL, COLS, N)
        )
    score_out[...] = jnp.broadcast_to(score, (K, N))


def renew_kernel(got, old, new, msg):
    out = lax.dot_general(
        got[:, W:], got[...], (((0,), (0,)), ((), ())), preferred_element_type=F32
    )
    total = out[0:8] + out[8:16] + out[16:24]
    fresh = (old[...] + total[:, :W]) / (1.0 + total[:, W + 32 : W + 33])
    fresh = fresh.astype(BF16)
    new[...] = fresh.astype(F32)
    msg[...] = jnp.broadcast_to(fresh[None], (TM, COLS, W))


def second_kernel(asg, res, asg_col, got, spec, right, left, rows, msg, score_out, tspec, srow, tiles):
    for p in range(PD):
        for r in range(RR):
            block = got[p * SL : (p + 1) * SL, :, r * N : (r + 1) * N].astype(F32)
            block = jnp.transpose(block, (1, 0, 2))
            tiles[:, p * N + r * SL : p * N + (r + 1) * SL, :] = block.astype(BF16)
    for c in range(COLS):
        both = transform_pair(tiles[c], right[...], left[...])
        tspec[c] = both[:, :N]
        tspec[COLS + c] = both[:, N:]
    score = score_patches(asg, res, rows, spec, tspec, srow)
    weight = 0.5 + 1.0 / (1.0 + jnp.exp(-score))
    lane = lax.broadcasted_iota(jnp.int32, (K, N), 1)
    at = lax.broadcasted_iota(jnp.int32, (K, N), 0) * COLS + asg_col[...]
    row = jnp.sum(jnp.where(lane == at, weight, 0.0), 0, keepdims=True)
    msg[...] = jnp.broadcast_to(row[None], (TM, 1, N))
    score_out[...] = jnp.broadcast_to(score, (K, N))


def last_kernel(ids, got, got_w, old, fin):
    count = TM * COLS
    row = lax.broadcasted_iota(jnp.int32, (count, N), 0)
    lane = lax.broadcasted_iota(jnp.int32, (count, N), 1)
    keep = (lane // COLS) == (row % COLS) + ids[0] * COLS
    pick = lax.broadcasted_iota(jnp.int32, (count, TM), 0) // COLS
    pick = (pick == lax.broadcasted_iota(jnp.int32, (count, TM), 1)).astype(BF16)
    out = jnp.zeros((N, W + N), F32)
    for piece in pieces(got_w[...]):
        part = jnp.dot(pick, piece.astype(BF16), preferred_element_type=F32)
        part = jnp.where(keep, part, 0.0).astype(BF16)
        out = out + lax.dot_general(
            part, got[...], (((0,), (0,)), ((), ())), preferred_element_type=F32
        )
    total = out[0:COLS]
    for m in range(1, N // COLS):
        total = total + out[m * COLS : (m + 1) * COLS]
    fresh = (old[...] + total[:, :W]) / (1.0 + total[:, W + 32 : W + 33])
    for c in range(COLS):
        parts = [fresh[c : c + 1, r * N : (r + 1) * N] for r in range(RR)]
        fin[c] = jnp.concatenate(parts, 0).astype(BF16)


def place_kernel(got, out):
    for p in range(PD):
        for g in range(COLS):
            block = got[p * SL : (p + 1) * SL, g * RR : (g + 1) * RR, :].astype(F32)
            block = jnp.transpose(block, (1, 0, 2)).reshape(N, N)
            out[PD * g + p] = block.astype(BF16)


def call(kernel, name, outs, ins, scratch, args, flops=1e8):
    spaces = {"s": pltpu.SMEM, "v": pltpu.VMEM}
    size = sum(int(np.prod(o.shape)) * o.dtype.itemsize for o in outs)
    return pl.pallas_call(
        kernel,
        name=name,
        out_shape=outs,
        in_specs=[pl.BlockSpec(memory_space=spaces[i]) for i in ins],
        out_specs=[pl.BlockSpec(memory_space=pltpu.VMEM) for _ in outs],
        scratch_shapes=scratch,
        compiler_params=pltpu.CompilerParams(vmem_limit_bytes=40 << 20),
        cost_estimate=pl.CostEstimate(flops=int(flops), bytes_accessed=size + (1 << 20), transcendentals=0),
    )(*args)


def struct(shape, dtype):
    return jax.ShapeDtypeStruct(shape, dtype)


def local(frames, offsets, assign, residual, template):
    right, left, rows = (jnp.asarray(t) for t in tables())
    off = offsets.reshape(PD, 2)
    asg = assign.reshape(K)
    res = residual.reshape(K, 2)
    col = assign.reshape(K, 1)
    t = lax.axis_index("tm").astype(jnp.int32)
    ids = jnp.stack([t // SL, t % SL])
    spec_shape = (K, 2 * N, N)
    temp = lax.all_to_all(
        template.reshape(COLS, PD * N, N), "plane", split_axis=0, concat_axis=0, tiled=True
    )
    spec, reg = call(
        prep_kernel,
        "prep",
        [struct(spec_shape, F32), struct((TM, COLS, W), BF16)],
        "ssvvv",
        [pltpu.VMEM((PD, N, COLS * N), F32), pltpu.VMEM((PD, COLS, N, N), F32)],
        (off, res, frames[0], right, left),
        flops=4e8,
    )
    msg, score_a, slab = call(
        first_kernel,
        "first",
        [struct((TM, COLS, W + N), BF16), struct((K, N), F32), struct((COLS, W), F32)],
        "sssvvvvvvv",
        [pltpu.VMEM(spec_shape, F32), pltpu.VMEM((K, N), F32), pltpu.VMEM((2 * N, N), F32)],
        (ids, asg, res, col, temp, spec, reg, right, left, rows),
        flops=4e8,
    )
    got = lax.all_to_all(
        msg.reshape(TM * COLS, W + N), "tm", split_axis=0, concat_axis=0, tiled=True
    )
    slab, msg = call(
        renew_kernel,
        "renew",
        [struct((COLS, W), F32), struct((TM, COLS, W), BF16)],
        "vv",
        [],
        (got, slab),
    )
    tiles = lax.all_to_all(msg, "tm", split_axis=0, concat_axis=0, tiled=True)
    msg, score_b = call(
        second_kernel,
        "second",
        [struct((TM, 1, N), F32), struct((K, N), F32)],
        "ssvvvvvv",
        [
            pltpu.VMEM(spec_shape, F32),
            pltpu.VMEM((K, N), F32),
            pltpu.VMEM((COLS, PD * N, N), BF16),
        ],
        (asg, res, col, tiles, spec, right, left, rows),
        flops=4e8,
    )
    got_w = lax.all_to_all(msg, "tm", split_axis=0, concat_axis=0, tiled=True).reshape(TM, N)
    (fin,) = call(
        last_kernel, "last", [struct((COLS, RR, N), BF16)], "svvv", [], (ids, got, got_w, slab)
    )
    fin = lax.all_to_all(fin, "plane", split_axis=0, concat_axis=0, tiled=True)
    msg = jnp.broadcast_to(fin.reshape(1, COLS * RR, N), (TM, COLS * RR, N))
    fin = lax.all_to_all(msg, "tm", split_axis=0, concat_axis=0, tiled=True)
    (out,) = call(place_kernel, "place", [struct((PD * COLS, N, N), BF16)], "v", [], (fin,))
    scores = jnp.stack([score_a[:, 0], score_b[:, 0]]).reshape(2, 1, PD, 1, COLS)
    return out, scores


def solution(mesh):
    return jax.shard_map(
        local,
        mesh=mesh,
        in_specs=(
            P("tm", "plane", None, None),
            P("tm", "plane", None),
            P("tm", "plane", None, None, None),
            P("tm", "plane", None, None, None),
            P(None, None, "plane"),
        ),
        out_specs=(P(None, None, "plane"), P(None, "tm", "plane", None, None)),
        check_vma=False,
    )
```

time: 453 us -> 142 us (0.31)
  blocking collectives: 245 us -> 84.9 us
  local copies, waits for them, and re-layouts: 50.1 us -> 6.85 us
  waiting for transfers between devices: 50 us -> 15.7 us
  starting transfers between devices: 46.6 us -> 15 us
  matrix products: 25.4 us -> 0 us
  other arithmetic: 20 us -> 2.01 us
  between operations: 14.5 us -> 0.71 us
  Pallas kernels: 0 us -> 13.7 us
    psum x2 -> x0, blocking collectives: 232 us -> none  [renew(): totals, weight_all = lax.psum((tile_sums, weight_sums), 'tm')]
    all_to_all x1 -> x4, blocking collectives: 13.4 us -> 84.9 us  [the longest x1 30.1 us: local(): lax.all_to_all(msg.reshape(TM * COLS, W + N), 'tm', split_axis=0, concat_...]
    psum x2 -> x0, waiting for transfers between devices: 37.4 us -> none  [renew(): totals, weight_all = lax.psum((tile_sums, weight_sums), 'tm')]
    all_to_all x3 -> x2, starting transfers between devices: 46.5 us -> 15 us  [the longest x1 10.4 us: local(): lax.all_to_all(template.reshape(COLS, PD * N, N), 'plane', split_axis=0,...]
    gather x22 -> x0, local copies, waits for them, and re-layouts: 29 us -> none  [the longest x2 9.64 us: cyclic(): lax.dynamic_slice_in_dim(doubled, (amount % length).astype(jnp.int32), le...]
    dot_general x31 -> x0, matrix products: 25.4 us -> none  [the longest x3 6.47 us: spectrum(): jnp.einsum('uy,nyk->nuk', sin_t, first_im, preferred_element_type=jnp.flo...]
    pallas_call x0 -> x6, Pallas kernels: none -> 13.7 us  [call(): pl.pallas_call(kernel, name=name, out_shape=outs, in_specs=[pl.BlockSpec(...]
    convert_element_type x8 -> x0, other arithmetic: 7 us -> none  [the longest x2 3.93 us: renew(): return ((old_rows_all.astype(jnp.float32) + totals) / (1.0 + jnp.repeat(w...]
  transfers between devices with their start and end apart: 5 -> 2, of which waited for: 3 -> 2; matrix products, arithmetic and copies ran while one was open for 6% -> 3% of each run, Pallas kernels for 0% -> 2%
where the time goes in v1:
time: 142 us; the launch traced here: 139 us
  blocking collectives  84.9 us (60%)
  waiting for transfers between devices  15.7 us (11%)
  starting transfers between devices  15 us (11%)
  Pallas kernels  13.7 us (10%)
  local copies, waits for them, and re-layouts  6.85 us (5%)
  other arithmetic  2.01 us (1%)
    all_to_all x1, blocking collectives, local(): lax.all_to_all(msg.reshape(TM * COLS, W + N), 'tm', split_axis=0, concat_...  30.1 us
    all_to_all x1, blocking collectives, local(): tiles = lax.all_to_all(msg, 'tm', split_axis=0, concat_axis=0, tiled=True)  24.4 us
    all_to_all x1, blocking collectives, local(): lax.all_to_all(msg, 'tm', split_axis=0, concat_axis=0, tiled=True)  18.3 us
    all_to_all x1, waiting for transfers between devices, local(): fin = lax.all_to_all(msg, 'tm', split_axis=0, concat_axis=0, tiled=True)  15.6 us
    pallas_call x6, Pallas kernels, call(): pl.pallas_call(kernel, name=name, out_shape=outs, in_specs=[pl.BlockSpec(...  13.7 us
    all_to_all x1, blocking collectives, local(): fin = lax.all_to_all(fin, 'plane', split_axis=0, concat_axis=0, tiled=True)  12.1 us
    all_to_all x1, starting transfers between devices, local(): lax.all_to_all(template.reshape(COLS, PD * N, N), 'plane', split_axis=0,...  10.4 us
    all_to_all x1, starting transfers between devices, local(): fin = lax.all_to_all(msg, 'tm', split_axis=0, concat_axis=0, tiled=True)  4.63 us
  transfers between devices with their start and end apart: 2, of which 2 were waited for; matrix products, arithmetic and copies ran while one was open for 3% of the time, Pallas kernels for 2%

profile of v1, /device:TPU:1, one launch (start us, length us, event | category | flops | bytes accessed | tf_op | source)
XLA Modules:
  0.0 139.0 jit_solution(15463105773364045696)
XLA Ops:
  0.7 10.4 %all-to-all-start = ((bf16[8,256,128]{2,1,0:T(8,128)(2,1)}), bf16[8,256,128]{2,1,0:T(8,128)(2,1)S(1)}, u32[]{:S(2)}, u32[]{:S(2)}) async-start(bf16[8,256,128]{2,1,0:T(8,128)(2,1)} %bitcast.20), calls=%async_computation | async-start | bytes 1048576 | tf_op jit(solution)/shard_map/all_to_all | solution.py:218
  11.0 0.5 broadcast.9
  11.6 1.3 reduce.9
  13.0 0.8 reshape.39.asg_col
  13.7 0.8 copy.33
  14.5 0.9 copy-done
  15.4 0.8 copy-done.3
  16.2 1.0 copy-done.5
  17.3 0.7 copy-done.6
  18.0 2.3 %prep.1 = (f32[16,256,128]{2,1,0:T(8,128)S(1)}, bf16[64,8,512]{2,1,0:T(8,128)(2,1)S(1)}) custom-call(s32[2,2]{1,0:T(2,128)S(1)} %bitcast.19, s32[16,2]{1,0:T(8,128)S(1)} %bitcast.15, bf16[2,128,1024]{2,1,0:T(8,128)(2,1)S(1)} %bitcast.18, bf16[128,256]{1,0:T(8,128)(2,1)S(1)} %copy-done.3, bf16[256,256]{1,0:T(8,128)(2,1)S(1)} %copy-done), custom_call_target="tpu_custom_call" | custom-call | flops 400000000 | bytes 3670016 | tf_op jit(solution)/shard_map/prep/pallas_call | solution.py:193
  20.3 0.1 all-to-all-done.temp
  20.4 4.2 %first.1 = (bf16[64,8,640]{2,1,0:T(8,128)(2,1)S(1)}, f32[16,128]{1,0:T(8,128)S(1)}, f32[8,512]{1,0:T(8,128)S(1)}) custom-call(s32[2]{0:T(128)S(1)} %pad_add_fusion.ids, s32[16]{0:T(128)S(1)} %reshape.33.asg, s32[16,2]{1,0:T(8,128)S(1)} %bitcast.16, s32[16,1]{1,0:T(8,128)S(1)} %reshape.39.asg_col, bf16[8,256,128]{2,1,0:T(8,128)(2,1)S(1)} %all-to-all-done.temp, ...), custom_call_target="tpu_custom_call" | custom-call | flops 400000000 | bytes 1728512 | tf_op jit(solution)/shard_map/first/pallas_call | solution.py:193
  24.6 30.1 %all_to_all.33 = bf16[64,8,640]{2,1,0:T(8,128)(2,1)S(1)} all-to-all(bf16[64,8,640]{2,1,0:T(8,128)(2,1)S(1)} %get-tuple-element.13), channel_id=1, replica_groups=mesh['tm'=64,'plane'=8] {'tm'}, dimensions={0} | all-to-all | bytes 1310720 | tf_op jit(solution)/shard_map/all_to_all | solution.py:239
  54.8 0.4 renew.1
  55.2 24.4 %all_to_all.34.got = bf16[64,8,512]{2,1,0:T(8,128)(2,1)S(1)} all-to-all(bf16[64,8,512]{2,1,0:T(8,128)(2,1)S(1)} %get-tuple-element.15), channel_id=1, replica_groups=mesh['tm'=64,'plane'=8] {'tm'}, dimensions={0} | all-to-all | bytes 1048576 | tf_op jit(solution)/shard_map/all_to_all | solution.py:250
  79.5 4.3 %second.1 = (f32[64,1,128]{2,1,0:T(1,128)S(1)}, f32[16,128]{1,0:T(8,128)S(1)}) custom-call(s32[16]{0:T(128)S(1)} %reshape.33.asg, s32[16,2]{1,0:T(8,128)S(1)} %bitcast.17, s32[16,1]{1,0:T(8,128)S(1)} %reshape.39.asg_col, bf16[64,8,512]{2,1,0:T(8,128)(2,1)S(1)} %all_to_all.34.got, f32[16,256,128]{2,1,0:T(8,128)S(1)} %get-tuple-element.11.spec, ...), custom_call_target="tpu_custom_call" | custom-call | flops 400000000 | bytes 1089536 | tf_op jit(solution)/shard_map/second/pallas_call | solution.py:193
  83.8 18.3 %all_to_all.35 = f32[64,1,128]{2,1,0:T(1,128)S(1)} all-to-all(f32[64,1,128]{2,1,0:T(1,128)S(1)} %get-tuple-element.16), channel_id=1, replica_groups=mesh['tm'=64,'plane'=8] {'tm'}, dimensions={0} | all-to-all | bytes 65536 | tf_op jit(solution)/shard_map/all_to_all | solution.py:264
  102.2 1.5 %last.1 = bf16[8,4,128]{2,1,0:T(4,128)(2,1)S(1)} custom-call(s32[2]{0:T(128)S(1)} %pad_add_fusion.ids, bf16[512,640]{1,0:T(8,128)(2,1)S(1)} %bitcast.13, f32[64,128]{1,0:T(8,128)S(1)} %bitcast.14, f32[8,512]{1,0:T(8,128)S(1)} %get-tuple-element.17.old), custom_call_target="tpu_custom_call" | custom-call | flops 100000000 | bytes 1056768 | tf_op jit(solution)/shard_map/last/pallas_call | solution.py:193
  103.7 12.1 %all_to_all.36 = bf16[8,4,128]{2,1,0:T(4,128)(2,1)S(1)} all-to-all(bf16[8,4,128]{2,1,0:T(4,128)(2,1)S(1)} %last.1), channel_id=1, replica_groups=mesh['tm'=64,'plane'=8] {'plane'}, dimensions={0} | all-to-all | bytes 16384 | tf_op jit(solution)/shard_map/all_to_all | solution.py:268
  115.8 0.9 broadcast_in_dim.8
  116.6 4.6 %all-to-all-start.5 = ((bf16[64,32,128]{2,1,0:T(8,128)(2,1)}), bf16[64,32,128]{2,1,0:T(8,128)(2,1)S(1)}, u32[]{:S(2)}, u32[]{:S(2)}) async-start(bf16[64,32,128]{2,1,0:T(8,128)(2,1)} %broadcast_in_dim.8), calls=%async_computation.5 | async-start | bytes 1048576 | tf_op jit(solution)/shard_map/all_to_all | solution.py:270
  121.7 0.6 pad_maximum_fusion
  122.3 15.6 %all-to-all-done.5.got = bf16[64,32,128]{2,1,0:T(8,128)(2,1)S(1)} async-done(((bf16[64,32,128]{2,1,0:T(8,128)(2,1)}), bf16[64,32,128]{2,1,0:T(8,128)(2,1)S(1)}, u32[]{:S(2)}, u32[]{:S(2)}) %all-to-all-start.5) | async-done | bytes 524320 | tf_op jit(solution)/shard_map/all_to_all | solution.py:270
  137.9 1.1 place.1
  (16 shorter events, 0.6 us)
Async XLA Ops:
  0.6 19.8 %copy-start.1 = (bf16[256,256]{1,0:T(8,128)(2,1)S(1)}, bf16[256,256]{1,0:T(8,128)(2,1)}, u32[]{:S(2)}) copy-start(bf16[256,256]{1,0:T(8,128)(2,1)} %constant.39.clone.left) | copy-start | bytes 393220
  0.6 19.8 %copy-start.4 = (bf16[128,256]{1,0:T(8,128)(2,1)S(1)}, bf16[128,256]{1,0:T(8,128)(2,1)}, u32[]{:S(2)}) copy-start(bf16[128,256]{1,0:T(8,128)(2,1)} %constant.38.clone.right) | copy-start | bytes 196612
  0.7 19.8 %copy-start.2 = (f32[128,256]{1,0:T(8,128)S(1)}, f32[128,256]{1,0:T(8,128)}, u32[]{:S(2)}) copy-start(f32[128,256]{1,0:T(8,128)} %constant.40.clone.rows) | copy-start | bytes 393220
  0.7 19.8 %all-to-all-start = ((bf16[8,256,128]{2,1,0:T(8,128)(2,1)}), bf16[8,256,128]{2,1,0:T(8,128)(2,1)S(1)}, u32[]{:S(2)}, u32[]{:S(2)}) async-start(bf16[8,256,128]{2,1,0:T(8,128)(2,1)} %bitcast.20), calls=%async_computation | async-start | bytes 1048576 | tf_op jit(solution)/shard_map/all_to_all | solution.py:218
  14.5 0.9 copy-start
  15.4 0.8 copy-start.3
  16.2 1.0 copy-start.5
  17.3 0.7 copy-start.6
  116.6 21.2 %all-to-all-start.5 = ((bf16[64,32,128]{2,1,0:T(8,128)(2,1)}), bf16[64,32,128]{2,1,0:T(8,128)(2,1)S(1)}, u32[]{:S(2)}, u32[]{:S(2)}) async-start(bf16[64,32,128]{2,1,0:T(8,128)(2,1)} %broadcast_in_dim.8), calls=%async_computation.5 | async-start | bytes 1048576 | tf_op jit(solution)/shard_map/all_to_all | solution.py:270

commit v2 on v1

--- a/solution.py
+++ b/solution.py
@@ -1,5 +1,3 @@
-import functools
-
 import jax
 import jax.numpy as jnp
 import numpy as np
@@ -60,8 +58,8 @@
             spec[k] = both[:, :N]
             spec[k + 1] = both[:, N:]
             for d, patch in ((0, one), (1, two)):
-                moved = pltpu.roll(patch, (-res[k + d, 0]) & (N - 1), 0)
-                regs[p, c + d] = pltpu.roll(moved, (-res[k + d, 1]) & (N - 1), 1)
+                moved = pltpu.roll(patch, (-res[p, 0, c + d]) & (N - 1), 0)
+                regs[p, c + d] = pltpu.roll(moved, (-res[p, 1, c + d]) & (N - 1), 1)
         for r in range(RR):
             block = regs[p, :, r * SL : (r + 1) * SL, :]
             block = jnp.transpose(block, (1, 0, 2))
@@ -70,7 +68,8 @@
 
 def score_patches(asg, res, rows, spec, tspec, srow):
     def one(k, carry):
-        tile = (k // COLS) * COLS + asg[k]
+        p, c = k // COLS, k % COLS
+        tile = p * COLS + asg[p, c]
         p_re, p_im = spec[k, :N, :], spec[k, N:, :]
         t_re, t_im = tspec[tile, :N, :], tspec[tile, N:, :]
         c_re = p_re * t_re + p_im * t_im
@@ -80,8 +79,8 @@
         scale = 1.0 / (modulus + 0.1 * level + 1e-06)
         n_re = (c_re * scale).astype(BF16)
         n_im = (c_im * scale).astype(BF16)
-        row_a = rows[pl.ds(res[k, 0] & (N - 1), 1), :]
-        row_b = rows[pl.ds(res[k, 1] & (N - 1), 1), :]
+        row_a = rows[pl.ds(res[p, 0, c] & (N - 1), 1), :]
+        row_b = rows[pl.ds(res[p, 1, c] & (N - 1), 1), :]
         lhs = jnp.concatenate([row_a[:, :N], row_a[:, N:]], 0).astype(BF16)
         s_re = jnp.dot(lhs, n_re, preferred_element_type=F32)
         s_im = jnp.dot(lhs, n_im, preferred_element_type=F32)
@@ -89,8 +88,16 @@
         srow[pl.ds(k, 1), :] = along
         return carry
 
-    lax.fori_loop(0, K, one, 0, unroll=2)
+    lax.fori_loop(0, K, one, 0, unroll=8)
     return jnp.sum(srow[...], 1, keepdims=True) * (1.0 / N)
+
+
+def column_of(asg):
+    row = lax.broadcasted_iota(jnp.int32, (K, 1), 0)
+    col = jnp.zeros((K, 1), jnp.int32)
+    for k in range(K):
+        col = jnp.where(row == k, asg[k // COLS, k % COLS], col)
+    return col
 
 
 def pieces(value):
@@ -100,7 +107,7 @@
     return high, mid, rest - mid
 
 
-def first_kernel(ids, asg, res, asg_col, temp, spec, reg_in, right, left, rows, msg, score_out, slab, tspec, srow, wide):
+def first_kernel(ids, asg, res, temp, spec, reg_in, right, left, rows, msg, score_out, slab, tspec, srow, wide):
     for c in range(COLS):
         both = transform_pair(temp[c], right[...], left[...])
         tspec[c] = both[:, :N]
@@ -113,7 +120,7 @@
     weight = 0.5 + 1.0 / (1.0 + jnp.exp(-score))
     high, mid, low = pieces(weight)
     lane = lax.broadcasted_iota(jnp.int32, (K, N), 1)
-    col = asg_col[...]
+    col = column_of(asg)
     meta = jnp.where(lane == 32, 1.0, 0.0)
     meta = jnp.where(lane == col, high, meta)
     meta = jnp.where(lane == col + 8, mid, meta)
@@ -137,7 +144,7 @@
     msg[...] = jnp.broadcast_to(fresh[None], (TM, COLS, W))
 
 
-def second_kernel(asg, res, asg_col, got, spec, right, left, rows, msg, score_out, tspec, srow, tiles):
+def second_kernel(asg, res, got, spec, right, left, rows, msg, score_out, tspec, srow, tiles):
     for p in range(PD):
         for r in range(RR):
             block = got[p * SL : (p + 1) * SL, :, r * N : (r + 1) * N].astype(F32)
@@ -150,7 +157,7 @@
     score = score_patches(asg, res, rows, spec, tspec, srow)
     weight = 0.5 + 1.0 / (1.0 + jnp.exp(-score))
     lane = lax.broadcasted_iota(jnp.int32, (K, N), 1)
-    at = lax.broadcasted_iota(jnp.int32, (K, N), 0) * COLS + asg_col[...]
+    at = lax.broadcasted_iota(jnp.int32, (K, N), 0) * COLS + column_of(asg)
     row = jnp.sum(jnp.where(lane == at, weight, 0.0), 0, keepdims=True)
     msg[...] = jnp.broadcast_to(row[None], (TM, 1, N))
     score_out[...] = jnp.broadcast_to(score, (K, N))
@@ -158,31 +165,32 @@
 
 def last_kernel(ids, got, got_w, old, fin):
     count = TM * COLS
-    row = lax.broadcasted_iota(jnp.int32, (count, N), 0)
-    lane = lax.broadcasted_iota(jnp.int32, (count, N), 1)
-    keep = (lane // COLS) == (row % COLS) + ids[0] * COLS
-    pick = lax.broadcasted_iota(jnp.int32, (count, TM), 0) // COLS
-    pick = (pick == lax.broadcasted_iota(jnp.int32, (count, TM), 1)).astype(BF16)
-    out = jnp.zeros((N, W + N), F32)
+    row = lax.broadcasted_iota(jnp.int32, (N, count), 0)
+    lane = lax.broadcasted_iota(jnp.int32, (N, count), 1)
+    keep = row // COLS == (lane & (COLS - 1)) + ids[0] * COLS
+    pick = lax.broadcasted_iota(jnp.int32, (TM, count), 1) // COLS
+    pick = (pick == lax.broadcasted_iota(jnp.int32, (TM, count), 0)).astype(BF16)
+    total = jnp.zeros((COLS, W + N), F32)
     for piece in pieces(got_w[...]):
-        part = jnp.dot(pick, piece.astype(BF16), preferred_element_type=F32)
-        part = jnp.where(keep, part, 0.0).astype(BF16)
-        out = out + lax.dot_general(
-            part, got[...], (((0,), (0,)), ((), ())), preferred_element_type=F32
+        part = lax.dot_general(
+            piece.astype(BF16), pick, (((0,), (0,)), ((), ())), preferred_element_type=F32
         )
-    total = out[0:COLS]
-    for m in range(1, N // COLS):
-        total = total + out[m * COLS : (m + 1) * COLS]
+        part = jnp.where(keep, part, 0.0)
+        spread = part[0:COLS]
+        for m in range(1, N // COLS):
+            spread = spread + part[m * COLS : (m + 1) * COLS]
+        total = total + jnp.dot(spread.astype(BF16), got[...], preferred_element_type=F32)
     fresh = (old[...] + total[:, :W]) / (1.0 + total[:, W + 32 : W + 33])
     for c in range(COLS):
         parts = [fresh[c : c + 1, r * N : (r + 1) * N] for r in range(RR)]
-        fin[c] = jnp.concatenate(parts, 0).astype(BF16)
+        tile = jnp.concatenate(parts, 0).astype(BF16)
+        fin[:, c] = jnp.broadcast_to(tile[None], (TM, RR, N))
 
 
 def place_kernel(got, out):
     for p in range(PD):
         for g in range(COLS):
-            block = got[p * SL : (p + 1) * SL, g * RR : (g + 1) * RR, :].astype(F32)
+            block = got[p * SL : (p + 1) * SL, g].astype(F32)
             block = jnp.transpose(block, (1, 0, 2)).reshape(N, N)
             out[PD * g + p] = block.astype(BF16)
 
@@ -209,9 +217,8 @@
 def local(frames, offsets, assign, residual, template):
     right, left, rows = (jnp.asarray(t) for t in tables())
     off = offsets.reshape(PD, 2)
-    asg = assign.reshape(K)
-    res = residual.reshape(K, 2)
-    col = assign.reshape(K, 1)
+    asg = assign.reshape(PD, COLS)
+    res = residual.reshape(PD, COLS, 2).transpose(0, 2, 1)
     t = lax.axis_index("tm").astype(jnp.int32)
     ids = jnp.stack([t // SL, t % SL])
     spec_shape = (K, 2 * N, N)
@@ -231,9 +238,9 @@
         first_kernel,
         "first",
         [struct((TM, COLS, W + N), BF16), struct((K, N), F32), struct((COLS, W), F32)],
-        "sssvvvvvvv",
+        "sssvvvvvv",
         [pltpu.VMEM(spec_shape, F32), pltpu.VMEM((K, N), F32), pltpu.VMEM((2 * N, N), F32)],
-        (ids, asg, res, col, temp, spec, reg, right, left, rows),
+        (ids, asg, res, temp, spec, reg, right, left, rows),
         flops=4e8,
     )
     got = lax.all_to_all(
@@ -252,22 +259,22 @@
         second_kernel,
         "second",
         [struct((TM, 1, N), F32), struct((K, N), F32)],
-        "ssvvvvvv",
+        "ssvvvvv",
         [
             pltpu.VMEM(spec_shape, F32),
             pltpu.VMEM((K, N), F32),
             pltpu.VMEM((COLS, PD * N, N), BF16),
         ],
-        (asg, res, col, tiles, spec, right, left, rows),
+        (asg, res, tiles, spec, right, left, rows),
         flops=4e8,
     )
     got_w = lax.all_to_all(msg, "tm", split_axis=0, concat_axis=0, tiled=True).reshape(TM, N)
     (fin,) = call(
-        last_kernel, "last", [struct((COLS, RR, N), BF16)], "svvv", [], (ids, got, got_w, slab)
-    )
-    fin = lax.all_to_all(fin, "plane", split_axis=0, concat_axis=0, tiled=True)
-    msg = jnp.broadcast_to(fin.reshape(1, COLS * RR, N), (TM, COLS * RR, N))
-    fin = lax.all_to_all(msg, "tm", split_axis=0, concat_axis=0, tiled=True)
+        last_kernel, "last", [struct((TM, COLS, RR, N), BF16)], "svvv", [], (ids, got, got_w, slab)
+    )
+    fin = lax.all_to_all(
+        fin.reshape(TM * COLS, RR, N), ("tm", "plane"), split_axis=0, concat_axis=0, tiled=True
+    ).reshape(TM, COLS, RR, N)
     (out,) = call(place_kernel, "place", [struct((PD * COLS, N, N), BF16)], "v", [], (fin,))
     scores = jnp.stack([score_a[:, 0], score_b[:, 0]]).reshape(2, 1, PD, 1, COLS)
     return out, scores

time: 142 us -> 137 us (0.965); the launches traced: 139 us -> 137 us
  blocking collectives: 84.9 us -> 72.9 us
  waiting for transfers between devices: 15.7 us -> 24.5 us
  starting transfers between devices: 15 us -> 21.6 us
  local copies, waits for them, and re-layouts: 6.85 us -> 4.57 us
  Pallas kernels: 13.7 us -> 11.7 us
    all_to_all x1 -> x0, blocking collectives: 12.1 us -> none  [local(): fin = lax.all_to_all(fin, 'plane', split_axis=0, concat_axis=0, tiled=True)]
    all_to_all x1, starting transfers between devices: 4.63 us -> 11.2 us  [local(): lax.all_to_all(fin.reshape(TM * COLS, RR, N), ('tm', 'plane'), split_axis...]
    all_to_all x1, waiting for transfers between devices: 15.6 us -> 21.5 us  [local(): lax.all_to_all(fin.reshape(TM * COLS, RR, N), ('tm', 'plane'), split_axis...]
    all_to_all x1, waiting for transfers between devices: 0.12 us -> 2.97 us  [local(): lax.all_to_all(template.reshape(COLS, PD * N, N), 'plane', split_axis=0,...]
    pallas_call x6, Pallas kernels: 13.7 us -> 11.7 us  [call(): pl.pallas_call(kernel, name=name, out_shape=outs, in_specs=[pl.BlockSpec(...]
    reshape x3 -> x0, local copies, waits for them, and re-layouts: 1.6 us -> none  [the longest x1 0.77 us: local(): res = residual.reshape(K, 2)]
    unnamed x15 -> x20, local copies, waits for them, and re-layouts: 3.99 us -> 4.17 us
  transfers between devices with their start and end apart: 2 -> 2, of which waited for: 2 -> 2; matrix products, arithmetic and copies ran while one was open for 3% -> 1% of each run, Pallas kernels for 2% -> 2%
where the time goes in v2:
time: 137 us
  blocking collectives  72.9 us (53%)
  waiting for transfers between devices  24.5 us (18%)
  starting transfers between devices  21.6 us (16%)
  Pallas kernels  11.7 us (9%)
  local copies, waits for them, and re-layouts  4.57 us (3%)
    all_to_all x1, blocking collectives, local(): lax.all_to_all(msg.reshape(TM * COLS, W + N), 'tm', split_axis=0, concat_...  30.1 us
    all_to_all x1, blocking collectives, local(): tiles = lax.all_to_all(msg, 'tm', split_axis=0, concat_axis=0, tiled=True)  24.5 us
    all_to_all x1, waiting for transfers between devices, local(): lax.all_to_all(fin.reshape(TM * COLS, RR, N), ('tm', 'plane'), split_axis...  21.5 us
    all_to_all x1, blocking collectives, local(): lax.all_to_all(msg, 'tm', split_axis=0, concat_axis=0, tiled=True)  18.3 us
    pallas_call x6, Pallas kernels, call(): pl.pallas_call(kernel, name=name, out_shape=outs, in_specs=[pl.BlockSpec(...  11.7 us
    all_to_all x1, starting transfers between devices, local(): lax.all_to_all(fin.reshape(TM * COLS, RR, N), ('tm', 'plane'), split_axis...  11.2 us
    all_to_all x1, starting transfers between devices, local(): lax.all_to_all(template.reshape(COLS, PD * N, N), 'plane', split_axis=0,...  10.4 us
    unnamed x20, local copies, waits for them, and re-layouts  4.17 us
  transfers between devices with their start and end apart: 2, of which 2 were waited for; matrix products, arithmetic and copies ran while one was open for 1% of the time, Pallas kernels for 2%

profile of v2, /device:TPU:1, one launch (start us, length us, event | category | flops | bytes accessed | tf_op | source)
XLA Modules:
  0.0 136.6 jit_solution(5215824272225320356)
XLA Ops:
  0.7 10.4 %all-to-all-start = ((bf16[8,256,128]{2,1,0:T(8,128)(2,1)}), bf16[8,256,128]{2,1,0:T(8,128)(2,1)S(1)}, u32[]{:S(2)}, u32[]{:S(2)}) async-start(bf16[8,256,128]{2,1,0:T(8,128)(2,1)} %bitcast.25), calls=%async_computation | async-start | bytes 1048576 | tf_op jit(solution)/shard_map/all_to_all | solution.py:225
  11.1 0.9 copy-done
  12.0 0.8 copy-done.3
  12.8 0.7 copy-done.5
  13.5 1.0 copy-done.8
  14.5 0.7 copy-done.9
  15.2 2.2 %prep.1 = (f32[16,256,128]{2,1,0:T(8,128)S(1)}, bf16[64,8,512]{2,1,0:T(8,128)(2,1)S(1)}) custom-call(s32[2,2]{1,0:T(2,128)S(1)} %bitcast.24, s32[2,2,8]{2,1,0:T(2,128)S(1)} %bitcast.18, bf16[2,128,1024]{2,1,0:T(8,128)(2,1)S(1)} %bitcast.23, bf16[128,256]{1,0:T(8,128)(2,1)S(1)} %copy-done.3, bf16[256,256]{1,0:T(8,128)(2,1)S(1)} %copy-done), custom_call_target="tpu_custom_call" | custom-call | flops 400000000 | bytes 3670016 | tf_op jit(solution)/shard_map/prep/pallas_call | solution.py:201
  17.4 0.1 pad_add_fusion.ids
  17.5 3.0 %all-to-all-done.temp = bf16[8,256,128]{2,1,0:T(8,128)(2,1)S(1)} async-done(((bf16[8,256,128]{2,1,0:T(8,128)(2,1)}), bf16[8,256,128]{2,1,0:T(8,128)(2,1)S(1)}, u32[]{:S(2)}, u32[]{:S(2)}) %all-to-all-start) | async-done | bytes 524320 | tf_op jit(solution)/shard_map/all_to_all | solution.py:225
  20.5 2.9 %first.1 = (bf16[64,8,640]{2,1,0:T(8,128)(2,1)S(1)}, f32[16,128]{1,0:T(8,128)S(1)}, f32[8,512]{1,0:T(8,128)S(1)}) custom-call(s32[2]{0:T(128)S(1)} %pad_add_fusion.ids, s32[2,8]{1,0:T(2,128)S(1)} %bitcast.21, s32[2,2,8]{2,1,0:T(2,128)S(1)} %bitcast.19, bf16[8,256,128]{2,1,0:T(8,128)(2,1)S(1)} %all-to-all-done.temp, ...), custom_call_target="tpu_custom_call" | custom-call | flops 400000000 | bytes 1728512 | tf_op jit(solution)/shard_map/first/pallas_call | solution.py:201
  23.3 30.1 %all_to_all.28 = bf16[64,8,640]{2,1,0:T(8,128)(2,1)S(1)} all-to-all(bf16[64,8,640]{2,1,0:T(8,128)(2,1)S(1)} %get-tuple-element.13), channel_id=1, replica_groups=mesh['tm'=64,'plane'=8] {'tm'}, dimensions={0} | all-to-all | bytes 1310720 | tf_op jit(solution)/shard_map/all_to_all | solution.py:246
  53.5 0.4 renew.1
  53.9 24.5 %all_to_all.29.got = bf16[64,8,512]{2,1,0:T(8,128)(2,1)S(1)} all-to-all(bf16[64,8,512]{2,1,0:T(8,128)(2,1)S(1)} %get-tuple-element.15), channel_id=1, replica_groups=mesh['tm'=64,'plane'=8] {'tm'}, dimensions={0} | all-to-all | bytes 1048576 | tf_op jit(solution)/shard_map/all_to_all | solution.py:257
  78.3 2.9 %second.1 = (f32[64,1,128]{2,1,0:T(1,128)S(1)}, f32[16,128]{1,0:T(8,128)S(1)}) custom-call(s32[2,8]{1,0:T(2,128)S(1)} %bitcast.22, s32[2,2,8]{2,1,0:T(2,128)S(1)} %bitcast.20, bf16[64,8,512]{2,1,0:T(8,128)(2,1)S(1)} %all_to_all.29.got, f32[16,256,128]{2,1,0:T(8,128)S(1)} %get-tuple-element.11.spec, bf16[128,256]{1,0:T(8,128)(2,1)S(1)} %copy-done.4, ...), custom_call_target="tpu_custom_call" | custom-call | flops 400000000 | bytes 1089536 | tf_op jit(solution)/shard_map/second/pallas_call | solution.py:201
  81.3 18.3 %all_to_all.30 = f32[64,1,128]{2,1,0:T(1,128)S(1)} all-to-all(f32[64,1,128]{2,1,0:T(1,128)S(1)} %get-tuple-element.16), channel_id=1, replica_groups=mesh['tm'=64,'plane'=8] {'tm'}, dimensions={0} | all-to-all | bytes 65536 | tf_op jit(solution)/shard_map/all_to_all | solution.py:271
  99.5 2.3 %last.1 = bf16[64,8,4,128]{3,2,1,0:T(4,128)(2,1)} custom-call(s32[2]{0:T(128)S(1)} %pad_add_fusion.ids, bf16[512,640]{1,0:T(8,128)(2,1)S(1)} %bitcast.15, f32[64,128]{1,0:T(8,128)S(1)} %bitcast.17, f32[8,512]{1,0:T(8,128)S(1)} %get-tuple-element.17.old), custom_call_target="tpu_custom_call" | custom-call | flops 100000000 | bytes 1572864 | tf_op jit(solution)/shard_map/last/pallas_call | solution.py:201
  101.8 11.2 %all-to-all-start.4 = ((bf16[512,4,128]{2,1,0:T(4,128)(2,1)}), bf16[512,4,128]{2,1,0:T(4,128)(2,1)S(1)}, u32[]{:S(2)}, u32[]{:S(2)}) async-start(bf16[512,4,128]{2,1,0:T(4,128)(2,1)} %bitcast.11), calls=%async_computation.4 | async-start | bytes 1048576 | tf_op jit(solution)/shard_map/all_to_all | solution.py:275
  113.0 0.1 slice_reduce_fusion.1
  113.1 0.1 stack.19
  113.2 0.1 slice_reduce_fusion
  113.3 0.1 stack.20
  113.4 0.6 pad_maximum_fusion
  114.0 21.5 %all-to-all-done.4 = bf16[512,4,128]{2,1,0:T(4,128)(2,1)S(1)} async-done(((bf16[512,4,128]{2,1,0:T(4,128)(2,1)}), bf16[512,4,128]{2,1,0:T(4,128)(2,1)S(1)}, u32[]{:S(2)}, u32[]{:S(2)}) %all-to-all-start.4) | async-done | bytes 524320 | tf_op jit(solution)/shard_map/all_to_all | solution.py:275
  135.5 1.1 place.1
  (15 shorter events, 0.0 us)
Async XLA Ops:
  0.6 19.8 %copy-start.1 = (bf16[256,256]{1,0:T(8,128)(2,1)S(1)}, bf16[256,256]{1,0:T(8,128)(2,1)}, u32[]{:S(2)}) copy-start(bf16[256,256]{1,0:T(8,128)(2,1)} %constant.39.clone.left) | copy-start | bytes 393220
  0.6 19.8 %copy-start.4 = (bf16[128,256]{1,0:T(8,128)(2,1)S(1)}, bf16[128,256]{1,0:T(8,128)(2,1)}, u32[]{:S(2)}) copy-start(bf16[128,256]{1,0:T(8,128)(2,1)} %constant.38.clone.right) | copy-start | bytes 196612
  0.7 19.8 %copy-start.2 = (f32[128,256]{1,0:T(8,128)S(1)}, f32[128,256]{1,0:T(8,128)}, u32[]{:S(2)}) copy-start(f32[128,256]{1,0:T(8,128)} %constant.40.clone.rows) | copy-start | bytes 393220
  0.7 19.8 %copy-start.6 = (s32[1,2,1,8,2]{3,4,2,1,0:T(2,128)S(1)}, s32[1,2,1,8,2]{3,4,2,1,0:T(2,128)}, u32[]{:S(2)}) copy-start(s32[1,2,1,8,2]{3,4,2,1,0:T(2,128)} %param.11) | copy-start | bytes 388
  0.7 19.8 %copy-start.7 = (s32[1,2,1,8,1]{3,4,2,1,0:T(1,128)S(1)}, s32[1,2,1,8,1]{3,4,2,1,0:T(1,128)}, u32[]{:S(2)}) copy-start(s32[1,2,1,8,1]{3,4,2,1,0:T(1,128)} %param.10) | copy-start | bytes 196
  0.7 19.8 %all-to-all-start = ((bf16[8,256,128]{2,1,0:T(8,128)(2,1)}), bf16[8,256,128]{2,1,0:T(8,128)(2,1)S(1)}, u32[]{:S(2)}, u32[]{:S(2)}) async-start(bf16[8,256,128]{2,1,0:T(8,128)(2,1)} %bitcast.25), calls=%async_computation | async-start | bytes 1048576 | tf_op jit(solution)/shard_map/all_to_all | solution.py:225
  11.1 0.9 copy-start
  12.0 0.8 copy-start.3
  12.8 0.7 copy-start.5
  13.5 1.0 copy-start.8
  14.5 0.7 copy-start.9
  101.8 33.7 %all-to-all-start.4 = ((bf16[512,4,128]{2,1,0:T(4,128)(2,1)}), bf16[512,4,128]{2,1,0:T(4,128)(2,1)S(1)}, u32[]{:S(2)}, u32[]{:S(2)}) async-start(bf16[512,4,128]{2,1,0:T(4,128)(2,1)} %bitcast.11), calls=%async_computation.4 | async-start | bytes 1048576 | tf_op jit(solution)/shard_map/all_to_all | solution.py:275

commit v3 on v1

v3 whole, which is shorter than its diff:
```python
import jax
import jax.numpy as jnp
import numpy as np
from jax import lax
from jax.experimental import pallas as pl
from jax.experimental.pallas import tpu as pltpu
from jax.sharding import PartitionSpec as P


N = 128
C = 8
PD = 2
CAP = 4
PAIRS = C * CAP // 2
ROWS = CAP * N + 16
SLAB = N // C
F32, BF16, I32 = jnp.float32, jnp.bfloat16, jnp.int32


def tables():
    j = np.arange(N, dtype=np.int32)
    phase = (j[:, None] * j[None, :] % N).astype(np.float32) * np.float32(2.0 * np.pi / N)
    cos = np.cos(phase).astype(BF16)
    sin = np.sin(phase).astype(BF16)
    right = np.concatenate([cos, -sin], 1)
    left = np.concatenate(
        [np.concatenate([cos, sin], 1), np.concatenate([-sin, cos], 1)], 0
    )
    rows = np.concatenate([cos, sin], 1)
    return right, left, rows


def dot(a, b):
    return jnp.dot(a, b, preferred_element_type=F32)


def transform_pair(pair, right, left):
    first = dot(pair, right).astype(BF16)
    inner = jnp.concatenate(
        [
            jnp.concatenate([first[:N, :N], first[N:, :N]], 1),
            jnp.concatenate([first[:N, N:], first[N:, N:]], 1),
        ],
        0,
    )
    return dot(left, inner)


def pieces(value):
    high = value.astype(BF16).astype(F32)
    rest = value - high
    mid = rest.astype(BF16).astype(F32)
    return high, mid, rest - mid


def iota(shape, axis):
    return lax.broadcasted_iota(I32, shape, axis)


def deal_kernel(off, asg, res, frames, out, shifted, details, count):
    out[...] = jnp.zeros_like(out)
    details[...] = jnp.zeros_like(details)
    for c in range(C):
        count[c] = 0
    for p in range(PD):
        plane = frames[p].astype(F32)
        plane = pltpu.roll(plane, (-off[p, 0]) & (N - 1), 0)
        plane = pltpu.roll(plane, (-off[p, 1]) & (C * N - 1), 1)
        shifted[p] = plane.astype(BF16)
    lane, row = iota((8, N), 1), iota((8, N), 0)
    for p in range(PD):
        for k in range(C):
            c = asg[p, k]
            slot = count[c]
            count[c] = slot + 1
            at = pl.multiple_of(slot * N, N)
            out[c, pl.ds(at, N), :] = shifted[p, :, k * N : (k + 1) * N]
            text = jnp.where(lane == 0, p, 0)
            text = jnp.where(lane == 1, res[p, 0, k], text)
            text = jnp.where(lane == 2, res[p, 1, k], text)
            text = jnp.where(lane == 3, 1, text)
            text = jnp.where(lane == 4, p * C + k, text).astype(F32)
            at = c * (CAP // 2) + slot // 2
            details[at] = jnp.where((row & 1) == (slot & 1), text, details[at])
    for c in range(C):
        for j in range(CAP // 2):
            out[c, CAP * N + 8 * j : CAP * N + 8 * (j + 1), :] = details[
                c * (CAP // 2) + j
            ].astype(BF16)


def tile_kernel(pair, right, left, spec):
    spec[...] = transform_pair(pair[...], right[...], left[...])


def along_of(both, tiles, info, phase):
    outs = []
    for e in range(2):
        p_re, p_im = both[:N, e * N : (e + 1) * N], both[N:, e * N : (e + 1) * N]
        upper = info[e : e + 1, 0:1] > 0.5
        t_re = jnp.where(upper, tiles[:N, N:], tiles[:N, :N])
        t_im = jnp.where(upper, tiles[N:, N:], tiles[N:, :N])
        c_re = p_re * t_re + p_im * t_im
        c_im = p_im * t_re - p_re * t_im
        modulus = jnp.sqrt(c_re * c_re + c_im * c_im)
        level = jnp.sum(jnp.sum(modulus, 0, keepdims=True), 1, keepdims=True) * (1.0 / (N * N))
        scale = 1.0 / (modulus + 0.1 * level + 1e-06)
        n_re = (c_re * scale).astype(BF16)
        n_im = (c_im * scale).astype(BF16)
        lhs = jnp.concatenate([phase[e : e + 1], phase[2 + e : 3 + e]], 0).astype(BF16)
        s_re, s_im = dot(lhs, n_re), dot(lhs, n_im)
        outs.append(
            phase[4 + e : 5 + e] * (s_re[0:1] - s_im[1:2])
            - phase[6 + e : 7 + e] * (s_re[1:2] + s_im[0:1])
        )
    return jnp.concatenate(outs, 0)


def match(spec, tiles, info, phase, along):
    along[...] = jnp.zeros_like(along)

    def one(i, carry):
        along[i, 0:2, :] = along_of(spec[i], tiles[...], info[i], phase[i])
        return carry

    lax.fori_loop(0, PAIRS, one, 0, unroll=8)


def weigh(along, info, w_low, w_high, turn):
    flat = info[...].reshape(C * 16, N)
    row = iota((C * 16, 1), 0)
    live = jnp.where((row & 7) < 2, flat[:, 3:4], 0.0)
    score = jnp.sum(along[...].reshape(C * 16, N), 1, keepdims=True) * (1.0 / N)
    weight = (0.5 + 1.0 / (1.0 + jnp.exp(-score))) * live
    high = weight * flat[:, 0:1]
    low = weight - high
    w_low[...] = jnp.broadcast_to(low, (C * 16, N)).reshape(PAIRS, 8, N)
    w_high[...] = jnp.broadcast_to(high, (C * 16, N)).reshape(PAIRS, 8, N)
    lane = iota((C * 16, N), 1)
    at = flat[:, 4:5].astype(I32) + turn * 16
    table = jnp.where(lane == at, score * live, 0.0).reshape(C, 16, N)
    return jnp.sum(table, 1), jnp.sum(low, 0, keepdims=True), jnp.sum(high, 0, keepdims=True)


def weighted(moved, w_low, w_high, low, high):
    def one(i, carry):
        low, high = carry
        wl, wh = w_low[i], w_high[i]
        for e in range(2):
            patch = moved[2 * i + e].astype(F32)
            low = low + patch * wl[e : e + 1]
            high = high + patch * wh[e : e + 1]
        return low, high

    return lax.fori_loop(0, PAIRS, one, (low, high), unroll=2)


def first_kernel(got, tiles, right, left, rows, msg, spec, moved, phase, info, table, along, w_low, w_high):
    flat = got[:, CAP * N :, :].astype(F32).reshape(C * 16, N)
    row, lane = iota((C * 16, N), 0), iota((C * 16, N), 1)
    info[...] = flat.reshape(PAIRS, 8, N)
    amount = jnp.where((row[:, 0:1] & 7) < 4, flat[:, 1:2], flat[:, 2:3]).astype(I32) & (N - 1)
    wave = dot((lane == amount).astype(BF16), rows[...])
    phase[...] = jnp.where((row & 3) < 2, wave[:, :N], wave[:, N:]).reshape(PAIRS, 8, N)

    def one(i, carry):
        at = pl.multiple_of((i % 2) * 2 * N, 2 * N)
        pair = got[i // 2, pl.ds(at, 2 * N), :]
        both = transform_pair(pair, right[...], left[...])
        spec[i] = both
        text = info[i]
        for e in range(2):
            down = (-text[e, 1].astype(I32)) & (N - 1)
            across = (-text[e, 2].astype(I32)) & (N - 1)
            patch = pltpu.roll(pair[e * N : (e + 1) * N].astype(F32), down, 0)
            moved[2 * i + e] = pltpu.roll(patch, across, 1).astype(BF16)
        return carry

    lax.fori_loop(0, PAIRS, one, 0, unroll=8)
    match(spec, tiles, info, phase, along)
    scores, low_sum, high_sum = weigh(along, info, w_low, w_high, 0)
    table[...] = scores
    zero = jnp.zeros((N, N), F32)
    low, high = weighted(moved, w_low, w_high, zero, zero)
    lines = [jnp.broadcast_to(v, (1, N)) for s in (low_sum, high_sum) for v in pieces(s)]
    tail = jnp.concatenate(lines + [jnp.zeros((10, N), F32)], 0).astype(BF16)
    low, high = low.astype(BF16), high.astype(BF16)
    for b in range(C):
        msg[b, :N, :] = low
        msg[b, N : 2 * N, :] = high
        msg[b, 2 * N :, :] = tail


def second_kernel(ids, got, old, spec, moved, phase, info, table, right, left, msg, tables_out, along, w_low, w_high, tiles):
    total = jnp.zeros((2 * N, N), F32)
    tail = jnp.zeros((16, N), F32)
    for b in range(C):
        total = total + got[b, : 2 * N, :].astype(F32)
        tail = tail + got[b, 2 * N :, :].astype(F32)
    fresh = []
    for p in range(PD):
        count = tail[3 * p : 3 * p + 1] + tail[3 * p + 1 : 3 * p + 2] + tail[3 * p + 2 : 3 * p + 3]
        part = old[p * N : (p + 1) * N, :].astype(F32) + total[p * N : (p + 1) * N]
        fresh.append((part / (1.0 + count)).astype(BF16))
    tiles[...] = transform_pair(jnp.concatenate(fresh, 0), right[...], left[...])
    match(spec, tiles, info, phase, along)
    scores, low_sum, high_sum = weigh(along, info, w_low, w_high, 1)
    tables_out[...] = table[...] + scores
    own = jnp.where(ids[0] == 0, 1.0, 0.0)
    low, high = weighted(
        moved, w_low, w_high, fresh[0].astype(F32) * own, fresh[1].astype(F32) * own
    )
    lines = [jnp.broadcast_to(s + own, (1, N)) for s in (low_sum, high_sum)]
    tail = jnp.concatenate(lines + [jnp.zeros((6, N), F32)], 0)
    msg[...] = jnp.zeros_like(msg)
    for b in range(C):
        at = ids[1] * C + b
        msg[at, :SLAB, :] = low[b * SLAB : (b + 1) * SLAB]
        msg[at, SLAB : 2 * SLAB, :] = high[b * SLAB : (b + 1) * SLAB]
        msg[at, 2 * SLAB :, :] = tail


def finish_kernel(ids, got, table, msg):
    total = got[ids[1] * C]
    for b in range(1, C):
        total = total + got[ids[1] * C + b]
    slab = jnp.concatenate(
        [
            total[p * SLAB : (p + 1) * SLAB] / total[2 * SLAB + p : 2 * SLAB + p + 1]
            for p in range(PD)
        ],
        0,
    ).astype(BF16)
    parts = pieces(table[...])
    pad = jnp.zeros((5, N), F32)
    for v in range(C):
        lines = jnp.concatenate([part[v : v + 1] for part in parts] + [pad], 0).astype(BF16)
        for y in range(C):
            msg[y * C + v, : 2 * SLAB, :] = slab
            msg[y * C + v, 2 * SLAB :, :] = lines


def place_kernel(ids, got, out, scores):
    for y in range(C):
        for g in range(C):
            for p in range(PD):
                out[PD * g + p, y * SLAB : (y + 1) * SLAB, :] = got[
                    y * C + g, p * SLAB : (p + 1) * SLAB, :
                ]
    total = jnp.zeros((8, N), F32)
    for c in range(C):
        total = total + got[ids[0] * C + c, 2 * SLAB :, :].astype(F32)
    scores[...] = total[0:1] + total[1:2] + total[2:3]


def call(kernel, outs, ins, scratch, args, flops=1e8):
    spaces = {"s": pltpu.SMEM, "v": pltpu.VMEM}
    size = sum(int(np.prod(o.shape)) * o.dtype.itemsize for o in outs)
    return pl.pallas_call(
        kernel,
        out_shape=outs,
        in_specs=[pl.BlockSpec(memory_space=spaces[i]) for i in ins],
        out_specs=[pl.BlockSpec(memory_space=pltpu.VMEM) for _ in outs],
        scratch_shapes=scratch,
        compiler_params=pltpu.CompilerParams(vmem_limit_bytes=40 << 20),
        cost_estimate=pl.CostEstimate(
            flops=int(flops), bytes_accessed=size + (1 << 20), transcendentals=0
        ),
    )(*args)


def struct(shape, dtype):
    return jax.ShapeDtypeStruct(shape, dtype)


def number(y, z, q):
    return (y * C + z) * C + q


def along_z():
    return [[y * C + z for z in range(C)] for y in range(C)]


def along_y():
    return [[y * C + z for y in range(C)] for z in range(C)]


def across():
    line = lambda z, q: [number(y, z, q) for y in range(C)]
    groups = [line(a, b) + line(b, a) for a in range(C) for b in range(a + 1, C)]
    return groups + [line(a, a) + line(a + 1, a + 1) for a in range(0, C, 2)]


def exchange(value, axis, groups=None):
    return lax.all_to_all(
        value, axis, split_axis=0, concat_axis=0, axis_index_groups=groups, tiled=True
    )


def local(frames, offsets, assign, residual, template):
    right, left, rows = (jnp.asarray(t) for t in tables())
    off = offsets.reshape(PD, 2)
    asg = assign.reshape(PD, C)
    res = residual.reshape(PD, C, 2).transpose(0, 2, 1)
    t = lax.axis_index("tm").astype(I32)
    q = lax.axis_index("plane").astype(I32)
    y, z = t >> 3, t & 7
    half = jnp.where(z == q, z & 1, (z < q).astype(I32))
    ids = jnp.stack([y, half])
    small = (PAIRS, 8, N)
    (dealt,) = call(
        deal_kernel,
        [struct((C, ROWS, N), BF16)],
        "sssv",
        [
            pltpu.VMEM((PD, N, C * N), BF16),
            pltpu.VMEM((C * CAP // 2, 8, N), F32),
            pltpu.SMEM((C,), I32),
        ],
        (off, asg, res, frames[0]),
    )
    got = exchange(dealt, "tm", along_z())
    swap = [
        (number(a, b, c), number(a, c, b)) for a in range(C) for b in range(C) for c in range(C)
    ]
    mine = lax.dynamic_slice_in_dim(template, PD * z, PD, 0).reshape(PD * N, N)
    old = lax.ppermute(mine, ("tm", "plane"), swap)
    (tiles,) = call(tile_kernel, [struct((2 * N, 2 * N), F32)], "vvv", [], (old, right, left))
    scratch = [pltpu.VMEM(small, F32) for _ in range(3)]
    msg, spec, moved, phase, info, table = call(
        first_kernel,
        [
            struct((C, 2 * N + 16, N), BF16),
            struct((PAIRS, 2 * N, 2 * N), F32),
            struct((2 * PAIRS, N, N), BF16),
            struct(small, F32),
            struct(small, F32),
            struct((C, N), F32),
        ],
        "vvvvv",
        scratch,
        (got, tiles, right, left, rows),
        flops=1e9,
    )
    got = exchange(msg, "tm", along_y())
    msg, table = call(
        second_kernel,
        [struct((2 * C, 2 * SLAB + 8, N), F32), struct((C, N), F32)],
        "svvvvvvvvv",
        scratch + [pltpu.VMEM((2 * N, 2 * N), F32)],
        (ids, got, old, spec, moved, phase, info, table, right, left),
        flops=1e9,
    )
    got = exchange(msg, ("tm", "plane"), across())
    (msg,) = call(
        finish_kernel, [struct((C * C, 2 * SLAB + 8, N), BF16)], "svv", [], (ids, got, table)
    )
    got = exchange(msg, "tm")
    out, scores = call(
        place_kernel, [struct((PD * C, N, N), BF16), struct((1, N), F32)], "sv", [], (ids, got)
    )
    return out, scores[0, : 2 * PD * C].reshape(2, 1, PD, 1, C)


def solution(mesh):
    return jax.shard_map(
        local,
        mesh=mesh,
        in_specs=(
            P("tm", "plane", None, None),
            P("tm", "plane", None),
            P("tm", "plane", None, None, None),
            P("tm", "plane", None, None, None),
            P(None, None, "plane"),
        ),
        out_specs=(P(None, None, "plane"), P(None, "tm", "plane", None, None)),
        check_vma=False,
    )
```

time: 142 us -> 141 us (level)
  the two profiles are of different devices: /device:TPU:1 before, /device:TPU:18 now
where the time goes in v3:
time: 141 us; the launch traced here: 140 us
  blocking collectives  55.5 us (39%)
  waiting for transfers between devices  38.4 us (27%)
  starting transfers between devices  22.7 us (16%)
  Pallas kernels  15.1 us (11%)
  local copies, waits for them, and re-layouts  7.99 us (6%)
    all_to_all x2, blocking collectives, exchange(): lax.all_to_all(value, axis, split_axis=0, concat_axis=0, axis_index_group...  55.5 us
    ppermute x1, waiting for transfers between devices, local(): old = lax.ppermute(mine, ('tm', 'plane'), swap)  24.2 us
    all_to_all x2, starting transfers between devices, exchange(): lax.all_to_all(value, axis, split_axis=0, concat_axis=0, axis_index_group...  17.9 us
    pallas_call x6, Pallas kernels, call(): pl.pallas_call(kernel, out_shape=outs, in_specs=[pl.BlockSpec(memory_spac...  15.1 us
    all_to_all x2, waiting for transfers between devices, exchange(): lax.all_to_all(value, axis, split_axis=0, concat_axis=0, axis_index_group...  14.2 us
    unnamed x20, local copies, waits for them, and re-layouts  7.29 us
    ppermute x1, starting transfers between devices, local(): old = lax.ppermute(mine, ('tm', 'plane'), swap)  4.79 us
  transfers between devices with their start and end apart: 3, of which 2 were waited for; matrix products, arithmetic and copies ran while one was open for 0% of the time, Pallas kernels for 0%

profile of v3, /device:TPU:18, one launch (start us, length us, event | category | flops | bytes accessed | tf_op | source)
XLA Modules:
  0.0 140.4 jit_solution(17691023990031738973)
XLA Ops:
  0.6 0.0 copy-start
  0.6 0.0 copy-start.3
  0.7 1.1 copy-done.3
  1.7 0.7 copy-done.6
  2.4 0.7 copy-done.7
  3.1 0.7 copy-done.8
  3.8 2.3 %shard_map.95 = bf16[8,528,128]{2,1,0:T(8,128)(2,1)} custom-call(s32[2,2]{1,0:T(2,128)S(1)} %bitcast.12, s32[2,8]{1,0:T(2,128)S(1)} %bitcast.13, s32[2,2,8]{2,1,0:T(2,128)S(1)} %bitcast.11, bf16[2,128,1024]{2,1,0:T(8,128)(2,1)S(1)} %bitcast.10), custom_call_target="tpu_custom_call" | custom-call | flops 100000000 | bytes 2129920 | tf_op jit(solution)/shard_map/pallas_call | solution.py:259
  6.1 10.4 %all-to-all-start = ((bf16[8,528,128]{2,1,0:T(8,128)(2,1)}), bf16[8,528,128]{2,1,0:T(8,128)(2,1)S(1)}, u32[]{:S(2)}, u32[]{:S(2)}) async-start(bf16[8,528,128]{2,1,0:T(8,128)(2,1)} %shard_map.95), calls=%async_computation | async-start | bytes 2162688 | tf_op jit(solution)/shard_map/all_to_all | solution.py:295
  16.6 4.8 %collective-permute-start = (bf16[256,128]{1,0:T(8,128)(2,1)S(1)}, bf16[256,128]{1,0:T(8,128)(2,1)S(1)}, u32[]{:S(2)}, u32[]{:S(2)}) collective-permute-start(bf16[256,128]{1,0:T(8,128)(2,1)S(1)} %bitcast.14), channel_id=1, source_target_pairs={{0,0},{1,8},{2,16},{3,24},{4,32},{5,40},{6,48},{7,56},{8,1},{9,9},... | collective-permute-start | bytes 196616 | tf_op jit(solution)/shard_map/ppermute | solution.py:327
  21.4 24.2 %collective-permute-done.pair.old = bf16[256,128]{1,0:T(8,128)(2,1)S(1)} collective-permute-done((bf16[256,128]{1,0:T(8,128)(2,1)S(1)}, bf16[256,128]{1,0:T(8,128)(2,1)S(1)}, u32[]{:S(2)}, u32[]{:S(2)}) %collective-permute-start) | collective-permute-done | bytes 65568 | tf_op jit(solution)/shard_map/ppermute | solution.py:327
  45.6 0.4 shard_map.96.tiles
  46.0 0.0 all-to-all-done.got
  46.0 6.3 %shard_map.97 = (bf16[8,272,128]{2,1,0:T(8,128)(2,1)}, f32[16,256,256]{2,1,0:T(8,128)S(1)}, bf16[32,128,128]{2,1,0:T(8,128)(2,1)S(1)}, f32[16,8,128]{2,1,0:T(8,1...) custom-call(bf16[8,528,128]{2,1,0:T(8,128)(2,1)S(1)} %all-to-all-done.got, f32[256,256]{1,0:T(8,128)S(1)} %shard_map.96.tiles, ...), custom_call_target="tpu_custom_call" | custom-call | flops 1000000000 | bytes 6983680 | tf_op jit(solution)/shard_map/pallas_call | solution.py:259
  52.3 2.0 %copy-done.1 = f32[16,256,256]{2,1,0:T(8,128)} copy-done((f32[16,256,256]{2,1,0:T(8,128)}, f32[16,256,256]{2,1,0:T(8,128)S(1)}, u32[]{:S(2)}) %copy-start.1) | copy-done | bytes 4194328
  54.3 7.4 %all-to-all-start.1 = ((bf16[8,272,128]{2,1,0:T(8,128)(2,1)}), bf16[8,272,128]{2,1,0:T(8,128)(2,1)S(1)}, u32[]{:S(2)}, u32[]{:S(2)}) async-start(bf16[8,272,128]{2,1,0:T(8,128)(2,1)} %get-tuple-element.12), calls=%async_computation.1 | async-start | bytes 1114112 | tf_op jit(solution)/shard_map/all_to_all | solution.py:295
  61.7 0.1 pad_add_fusion.ids
  61.8 14.2 %all-to-all-done.1.got = bf16[8,272,128]{2,1,0:T(8,128)(2,1)S(1)} async-done(((bf16[8,272,128]{2,1,0:T(8,128)(2,1)}), bf16[8,272,128]{2,1,0:T(8,128)(2,1)S(1)}, u32[]{:S(2)}, u32[]{:S(2)}) %all-to-all-start.1) | async-done | bytes 557088 | tf_op jit(solution)/shard_map/all_to_all | solution.py:295
  76.0 2.2 %copy-done.2 = f32[16,256,256]{2,1,0:T(8,128)S(1)} copy-done((f32[16,256,256]{2,1,0:T(8,128)S(1)}, f32[16,256,256]{2,1,0:T(8,128)}, u32[]{:S(2)}) %copy-start.2) | copy-done | bytes 4194328
  78.2 4.1 %shard_map.98 = (f32[16,40,128]{2,1,0:T(8,128)S(1)}, f32[8,128]{1,0:T(8,128)S(1)}) custom-call(s32[2]{0:T(128)S(1)} %pad_add_fusion.ids, bf16[8,272,128]{2,1,0:T(8,128)(2,1)S(1)} %all-to-all-done.1.got, bf16[256,128]{1,0:T(8,128)(2,1)S(1)} %collective-permute-done.pair.old, f32[16,256,256]{2,1,0:T(8,128)S(1)} %copy-done.2, ...), custom_call_target="tpu_custom_call" | custom-call | flops 1000000000 | bytes 1380352 | tf_op jit(solution)/shard_map/pallas_call | solution.py:259
  82.3 21.9 %all_to_all.20.got = f32[16,40,128]{2,1,0:T(8,128)S(1)} all-to-all(f32[16,40,128]{2,1,0:T(8,128)S(1)} %get-tuple-element.18), channel_id=1, replica_groups={{1,65,129,193,257,321,385,449,8,72,136,200,264,328,392,456},{2,66,130,1..., dimensions={0} | all-to-all | bytes 655360 | tf_op jit(solution)/shard_map/all_to_all | solution.py:295
  104.2 0.6 shard_map.99
  104.8 33.6 %all_to_all.21.got = bf16[64,40,128]{2,1,0:T(8,128)(2,1)S(1)} all-to-all(bf16[64,40,128]{2,1,0:T(8,128)(2,1)S(1)} %shard_map.99), channel_id=1, replica_groups=mesh['tm'=64,'plane'=8] {'tm'}, dimensions={0} | all-to-all | bytes 1310720 | tf_op jit(solution)/shard_map/all_to_all | solution.py:295
  138.4 1.4 shard_map.100
  139.8 0.7 reshape_squeeze.3
  (14 shorter events, 0.1 us)
Async XLA Ops:
  0.6 16.0 %copy-start = (bf16[16,128,128]{2,1,0:T(8,128)(2,1)S(1)}, bf16[16,128,128]{2,1,0:T(8,128)(2,1)}, u32[]{:S(2)}) copy-start(bf16[16,128,128]{2,1,0:T(8,128)(2,1)} %param.12) | copy-start | bytes 1572868
  0.6 1.1 copy-start.3
  1.7 0.7 copy-start.6
  2.4 0.7 copy-start.7
  3.1 0.7 copy-start.8
  6.1 39.5 %copy-start.4 = (bf16[256,256]{1,0:T(8,128)(2,1)S(1)}, bf16[256,256]{1,0:T(8,128)(2,1)}, u32[]{:S(2)}) copy-start(bf16[256,256]{1,0:T(8,128)(2,1)} %constant.28.clone.left) | copy-start | bytes 393220
  6.1 39.5 %copy-start.5 = (bf16[128,256]{1,0:T(8,128)(2,1)S(1)}, bf16[128,256]{1,0:T(8,128)(2,1)}, u32[]{:S(2)}) copy-start(bf16[128,256]{1,0:T(8,128)(2,1)} %constant.27.clone.right) | copy-start | bytes 196612
  6.1 39.9 %copy-start.9 = (bf16[128,256]{1,0:T(8,128)(2,1)S(1)}, bf16[128,256]{1,0:T(8,128)(2,1)}, u32[]{:S(2)}) copy-start(bf16[128,256]{1,0:T(8,128)(2,1)} %constant.29.clone.rows) | copy-start | bytes 196612
  6.1 39.9 %all-to-all-start = ((bf16[8,528,128]{2,1,0:T(8,128)(2,1)}), bf16[8,528,128]{2,1,0:T(8,128)(2,1)S(1)}, u32[]{:S(2)}, u32[]{:S(2)}) async-start(bf16[8,528,128]{2,1,0:T(8,128)(2,1)} %shard_map.95), calls=%async_computation | async-start | bytes 2162688 | tf_op jit(solution)/shard_map/all_to_all | solution.py:295
  16.6 29.0 %collective-permute-start = (bf16[256,128]{1,0:T(8,128)(2,1)S(1)}, bf16[256,128]{1,0:T(8,128)(2,1)S(1)}, u32[]{:S(2)}, u32[]{:S(2)}) collective-permute-start(bf16[256,128]{1,0:T(8,128)(2,1)S(1)} %bitcast.14), channel_id=1, source_target_pairs={{0,0},{1,8},{2,16},{3,24},{4,32},{5,40},{6,48},{7,56},{8,1},{9,9},... | collective-permute-start | bytes 196616 | tf_op jit(solution)/shard_map/ppermute | solution.py:327
  52.3 2.0 %copy-start.1 = (f32[16,256,256]{2,1,0:T(8,128)}, f32[16,256,256]{2,1,0:T(8,128)S(1)}, u32[]{:S(2)}) copy-start(f32[16,256,256]{2,1,0:T(8,128)S(1)} %get-tuple-element.13.spec) | copy-start | bytes 12582916
  54.3 21.7 %all-to-all-start.1 = ((bf16[8,272,128]{2,1,0:T(8,128)(2,1)}), bf16[8,272,128]{2,1,0:T(8,128)(2,1)S(1)}, u32[]{:S(2)}, u32[]{:S(2)}) async-start(bf16[8,272,128]{2,1,0:T(8,128)(2,1)} %get-tuple-element.12), calls=%async_computation.1 | async-start | bytes 1114112 | tf_op jit(solution)/shard_map/all_to_all | solution.py:295
  76.0 2.2 %copy-start.2 = (f32[16,256,256]{2,1,0:T(8,128)S(1)}, f32[16,256,256]{2,1,0:T(8,128)}, u32[]{:S(2)}) copy-start(f32[16,256,256]{2,1,0:T(8,128)} %copy-done.1) | copy-start | bytes 12582916

commit v4 on v3

--- a/solution.py
+++ b/solution.py
@@ -57,11 +57,21 @@
     return lax.broadcasted_iota(I32, shape, axis)
 
 
-def deal_kernel(off, asg, res, frames, out, shifted, details, count):
+def deal_kernel(ids, off_in, asg_in, res_in, frames_in, out, frames, off, asg, res, shifted, details, count, sems):
+    copies = [
+        pltpu.make_async_copy(source, target, sems.at[i])
+        for i, (source, target) in enumerate(
+            ((off_in, off), (asg_in, asg), (res_in, res), (frames_in, frames))
+        )
+    ]
+    for copy in copies:
+        copy.start()
     out[...] = jnp.zeros_like(out)
     details[...] = jnp.zeros_like(details)
     for c in range(C):
         count[c] = 0
+    for copy in copies:
+        copy.wait()
     for p in range(PD):
         plane = frames[p].astype(F32)
         plane = pltpu.roll(plane, (-off[p, 0]) & (N - 1), 0)
@@ -70,7 +80,7 @@
     lane, row = iota((8, N), 1), iota((8, N), 0)
     for p in range(PD):
         for k in range(C):
-            c = asg[p, k]
+            c = (asg[p, k] + ids[2]) & (C - 1)
             slot = count[c]
             count[c] = slot + 1
             at = pl.multiple_of(slot * N, N)
@@ -242,19 +252,22 @@
 
 def place_kernel(ids, got, out, scores):
     for y in range(C):
-        for g in range(C):
+        for z in range(C):
+            group = (z - ids[2]) & (C - 1)
             for p in range(PD):
-                out[PD * g + p, y * SLAB : (y + 1) * SLAB, :] = got[
-                    y * C + g, p * SLAB : (p + 1) * SLAB, :
+                out[PD * group + p, y * SLAB : (y + 1) * SLAB, :] = got[
+                    y * C + z, p * SLAB : (p + 1) * SLAB, :
                 ]
     total = jnp.zeros((8, N), F32)
     for c in range(C):
         total = total + got[ids[0] * C + c, 2 * SLAB :, :].astype(F32)
-    scores[...] = total[0:1] + total[1:2] + total[2:3]
-
-
-def call(kernel, outs, ins, scratch, args, flops=1e8):
-    spaces = {"s": pltpu.SMEM, "v": pltpu.VMEM}
+    line = total[0:1] + total[1:2] + total[2:3]
+    for j in range(2 * PD):
+        scores[j // PD, 0, j % PD, :, :] = line[:, j * C : (j + 1) * C]
+
+
+def call(kernel, outs, ins, scratch, args, flops=1e8, grant=16):
+    spaces = {"s": pltpu.SMEM, "v": pltpu.VMEM, "h": pltpu.HBM}
     size = sum(int(np.prod(o.shape)) * o.dtype.itemsize for o in outs)
     return pl.pallas_call(
         kernel,
@@ -262,7 +275,7 @@
         in_specs=[pl.BlockSpec(memory_space=spaces[i]) for i in ins],
         out_specs=[pl.BlockSpec(memory_space=pltpu.VMEM) for _ in outs],
         scratch_shapes=scratch,
-        compiler_params=pltpu.CompilerParams(vmem_limit_bytes=40 << 20),
+        compiler_params=pltpu.CompilerParams(vmem_limit_bytes=grant << 20),
         cost_estimate=pl.CostEstimate(
             flops=int(flops), bytes_accessed=size + (1 << 20), transcendentals=0
         ),
@@ -286,9 +299,14 @@
 
 
 def across():
-    line = lambda z, q: [number(y, z, q) for y in range(C)]
-    groups = [line(a, b) + line(b, a) for a in range(C) for b in range(a + 1, C)]
-    return groups + [line(a, a) + line(a + 1, a + 1) for a in range(0, C, 2)]
+    groups = []
+    for z in range(C):
+        pairs = [(a, (z - a) % C) for a in range(C) if a < (z - a) % C]
+        if z % 2 == 0:
+            pairs.append((z // 2, z // 2 + C // 2))
+        for pair in pairs:
+            groups.append([number(y, z, q) for q in pair for y in range(C)])
+    return groups
 
 
 def exchange(value, axis, groups=None):
@@ -305,25 +323,35 @@
     t = lax.axis_index("tm").astype(I32)
     q = lax.axis_index("plane").astype(I32)
     y, z = t >> 3, t & 7
-    half = jnp.where(z == q, z & 1, (z < q).astype(I32))
-    ids = jnp.stack([y, half])
+    other = (z - q) & (C - 1)
+    half = jnp.where(other == q, q >> 2, (q < other).astype(I32))
+    ids = jnp.stack([y, half, q])
     small = (PAIRS, 8, N)
     (dealt,) = call(
         deal_kernel,
         [struct((C, ROWS, N), BF16)],
-        "sssv",
+        "shhhh",
         [
+            pltpu.VMEM((PD, N, C * N), BF16),
+            pltpu.SMEM((PD, 2), I32),
+            pltpu.SMEM((PD, C), I32),
+            pltpu.SMEM((PD, 2, C), I32),
             pltpu.VMEM((PD, N, C * N), BF16),
             pltpu.VMEM((C * CAP // 2, 8, N), F32),
             pltpu.SMEM((C,), I32),
+            pltpu.SemaphoreType.DMA((4,)),
         ],
-        (off, asg, res, frames[0]),
+        (ids, off, asg, res, frames[0]),
+        grant=63,
     )
     got = exchange(dealt, "tm", along_z())
     swap = [
-        (number(a, b, c), number(a, c, b)) for a in range(C) for b in range(C) for c in range(C)
+        (number(a, b, c), number(a, b, (b - c) % C))
+        for a in range(C)
+        for b in range(C)
+        for c in range(C)
     ]
-    mine = lax.dynamic_slice_in_dim(template, PD * z, PD, 0).reshape(PD * N, N)
+    mine = lax.dynamic_slice_in_dim(template, PD * other, PD, 0).reshape(PD * N, N)
     old = lax.ppermute(mine, ("tm", "plane"), swap)
     (tiles,) = call(tile_kernel, [struct((2 * N, 2 * N), F32)], "vvv", [], (old, right, left))
     scratch = [pltpu.VMEM(small, F32) for _ in range(3)]
@@ -357,9 +385,13 @@
     )
     got = exchange(msg, "tm")
     out, scores = call(
-        place_kernel, [struct((PD * C, N, N), BF16), struct((1, N), F32)], "sv", [], (ids, got)
-    )
-    return out, scores[0, : 2 * PD * C].reshape(2, 1, PD, 1, C)
+        place_kernel,
+        [struct((PD * C, N, N), BF16), struct((2, 1, PD, 1, C), F32)],
+        "sv",
+        [],
+        (ids, got),
+    )
+    return out, scores
 
 
 def solution(mesh):

time: 141 us -> 125 us (0.89)
  the two profiles are of different devices: /device:TPU:18 before, /device:TPU:16 now
where the time goes in v4:
time: 125 us
  blocking collectives  68.4 us (55%)
  waiting for transfers between devices  28.3 us (23%)
  Pallas kernels  15.5 us (12%)
  starting transfers between devices  11.1 us (9%)
    all_to_all x3, blocking collectives, exchange(): lax.all_to_all(value, axis, split_axis=0, concat_axis=0, axis_index_group...  68.4 us
    all_to_all x1, waiting for transfers between devices, exchange(): lax.all_to_all(value, axis, split_axis=0, concat_axis=0, axis_index_group...  28.3 us
    pallas_call x6, Pallas kernels, call(): pl.pallas_call(kernel, out_shape=outs, in_specs=[pl.BlockSpec(memory_spac...  15.5 us
    all_to_all x1, starting transfers between devices, exchange(): lax.all_to_all(value, axis, split_axis=0, concat_axis=0, axis_index_group...  10.5 us
  transfers between devices with their start and end apart: 2, of which 1 were waited for; matrix products, arithmetic and copies ran while one was open for 0% of the time, Pallas kernels for 0%

profile of v4, /device:TPU:16, one launch (start us, length us, event | category | flops | bytes accessed | tf_op | source)
XLA Modules:
  0.0 124.7 jit_solution(3608185264872450900)
XLA Ops:
  0.6 0.0 copy-start
  0.7 0.6 pad_add_fusion.ids
  1.2 3.3 %shard_map.95 = bf16[8,528,128]{2,1,0:T(8,128)(2,1)} custom-call(s32[3]{0:T(128)} %pad_add_fusion.ids, s32[2,2]{1,0:T(2,128)} %bitcast.13, s32[2,8]{1,0:T(2,128)} %bitcast.14, s32[2,2,8]{2,1,0:T(2,128)} %bitcast.12, bf16[2,128,1024]{2,1,0:T(8,128)(2,1)} %bitcast.10), custom_call_target="tpu_custom_call" | custom-call | flops 100000000 | bytes 2129920 | tf_op jit(solution)/shard_map/pallas_call | solution.py:272
  4.6 0.0 copy-start.1
  4.6 0.0 copy-start.2
  4.6 0.0 copy-start.4
  4.6 10.5 %all-to-all-start = ((bf16[8,528,128]{2,1,0:T(8,128)(2,1)}), bf16[8,528,128]{2,1,0:T(8,128)(2,1)S(1)}, u32[]{:S(2)}, u32[]{:S(2)}) async-start(bf16[8,528,128]{2,1,0:T(8,128)(2,1)} %shard_map.95), calls=%async_computation | async-start | bytes 2162688 | tf_op jit(solution)/shard_map/all_to_all | solution.py:313
  15.1 0.0 copy-done
  15.1 0.7 collective-permute-start
  15.8 0.0 collective-permute-done.pair.old
  15.8 0.0 copy-done.1
  15.8 0.0 copy-done.2
  15.8 0.4 shard_map.96.tiles
  16.2 28.3 %all-to-all-done.got = bf16[8,528,128]{2,1,0:T(8,128)(2,1)S(1)} async-done(((bf16[8,528,128]{2,1,0:T(8,128)(2,1)}), bf16[8,528,128]{2,1,0:T(8,128)(2,1)S(1)}, u32[]{:S(2)}, u32[]{:S(2)}) %all-to-all-start) | async-done | bytes 1081376 | tf_op jit(solution)/shard_map/all_to_all | solution.py:313
  44.5 0.0 copy-done.4
  44.5 5.5 %shard_map.97 = (bf16[8,272,128]{2,1,0:T(8,128)(2,1)S(1)}, f32[16,256,256]{2,1,0:T(8,128)S(1)}, bf16[32,128,128]{2,1,0:T(8,128)(2,1)S(1)}, f32[16,8,128]{2,1,0:T...) custom-call(bf16[8,528,128]{2,1,0:T(8,128)(2,1)S(1)} %all-to-all-done.got, f32[256,256]{1,0:T(8,128)S(1)} %shard_map.96.tiles, ...), custom_call_target="tpu_custom_call" | custom-call | flops 1000000000 | bytes 6983680 | tf_op jit(solution)/shard_map/pallas_call | solution.py:272
  50.1 0.0 copy-start.3
  50.1 23.2 %all_to_all.20.got = bf16[8,272,128]{2,1,0:T(8,128)(2,1)S(1)} all-to-all(bf16[8,272,128]{2,1,0:T(8,128)(2,1)S(1)} %get-tuple-element.10), channel_id=1, replica_groups={{0,64,128,192,256,320,384,448},{8,72,136,200,264,328,392,456},{16,80,14..., dimensions={0} | all-to-all | bytes 1114112 | tf_op jit(solution)/shard_map/all_to_all | solution.py:313
  73.3 0.0 copy-done.3
  73.3 4.2 %shard_map.98 = (f32[16,40,128]{2,1,0:T(8,128)S(1)}, f32[8,128]{1,0:T(8,128)S(1)}) custom-call(s32[3]{0:T(128)S(1)} %copy-done.3, bf16[8,272,128]{2,1,0:T(8,128)(2,1)S(1)} %all_to_all.20.got, bf16[256,128]{1,0:T(8,128)(2,1)S(1)} %collective-permute-done.pair.old, f32[16,256,256]{2,1,0:T(8,128)S(1)} %get-tuple-element.11.spec, ...), custom_call_target="tpu_custom_call" | custom-call | flops 1000000000 | bytes 1380352 | tf_op jit(solution)/shard_map/pallas_call | solution.py:272
  77.5 16.5 %all_to_all.21.got = f32[16,40,128]{2,1,0:T(8,128)S(1)} all-to-all(f32[16,40,128]{2,1,0:T(8,128)S(1)} %get-tuple-element.16), channel_id=1, replica_groups={{1,65,129,193,257,321,385,449,7,71,135,199,263,327,391,455},{2,66,130,1..., dimensions={0} | all-to-all | bytes 655360 | tf_op jit(solution)/shard_map/all_to_all | solution.py:313
  94.0 0.6 shard_map.99
  94.6 28.7 %all_to_all.22.got = bf16[64,40,128]{2,1,0:T(8,128)(2,1)S(1)} all-to-all(bf16[64,40,128]{2,1,0:T(8,128)(2,1)S(1)} %shard_map.99), channel_id=1, replica_groups=mesh['tm'=64,'plane'=8] {'tm'}, dimensions={0} | all-to-all | bytes 1310720 | tf_op jit(solution)/shard_map/all_to_all | solution.py:313
  123.3 1.4 %shard_map.100 = (bf16[16,128,128]{2,1,0:T(8,128)(2,1)}, f32[2,1,2,1,8]{4,3,2,1,0:T(1,128)}) custom-call(s32[3]{0:T(128)S(1)} %copy-done.3, bf16[64,40,128]{2,1,0:T(8,128)(2,1)S(1)} %all_to_all.22.got), custom_call_target="tpu_custom_call" | custom-call | flops 100000000 | bytes 1572992 | tf_op jit(solution)/shard_map/pallas_call | solution.py:272
  (1 shorter events, 0.0 us)
Async XLA Ops:
  0.6 14.5 %copy-start = (bf16[16,128,128]{2,1,0:T(8,128)(2,1)S(1)}, bf16[16,128,128]{2,1,0:T(8,128)(2,1)}, u32[]{:S(2)}) copy-start(bf16[16,128,128]{2,1,0:T(8,128)(2,1)} %param.12) | copy-start | bytes 1572868
  4.6 11.2 %copy-start.1 = (bf16[256,256]{1,0:T(8,128)(2,1)S(1)}, bf16[256,256]{1,0:T(8,128)(2,1)}, u32[]{:S(2)}) copy-start(bf16[256,256]{1,0:T(8,128)(2,1)} %constant.26.clone.left) | copy-start | bytes 393220
  4.6 11.2 %copy-start.2 = (bf16[128,256]{1,0:T(8,128)(2,1)S(1)}, bf16[128,256]{1,0:T(8,128)(2,1)}, u32[]{:S(2)}) copy-start(bf16[128,256]{1,0:T(8,128)(2,1)} %constant.25.clone.right) | copy-start | bytes 196612
  4.6 39.9 %copy-start.4 = (bf16[128,256]{1,0:T(8,128)(2,1)S(1)}, bf16[128,256]{1,0:T(8,128)(2,1)}, u32[]{:S(2)}) copy-start(bf16[128,256]{1,0:T(8,128)(2,1)} %constant.27.clone.rows) | copy-start | bytes 196612
  4.6 39.9 %all-to-all-start = ((bf16[8,528,128]{2,1,0:T(8,128)(2,1)}), bf16[8,528,128]{2,1,0:T(8,128)(2,1)S(1)}, u32[]{:S(2)}, u32[]{:S(2)}) async-start(bf16[8,528,128]{2,1,0:T(8,128)(2,1)} %shard_map.95), calls=%async_computation | async-start | bytes 2162688 | tf_op jit(solution)/shard_map/all_to_all | solution.py:313
  15.1 0.7 collective-permute-start
  50.1 23.2 %copy-start.3 = (s32[3]{0:T(128)S(1)}, s32[3]{0:T(128)}, u32[]{:S(2)}) copy-start(s32[3]{0:T(128)} %pad_add_fusion.ids) | copy-start | bytes 40

commit v5 on v4

--- a/solution.py
+++ b/solution.py
@@ -53,11 +53,22 @@
     return high, mid, rest - mid
 
 
+def place():
+    t = lax.axis_index("tm").astype(I32)
+    return t >> 3, t & (C - 1), lax.axis_index("plane").astype(I32)
+
+
+def own_half():
+    _, z, q = place()
+    other = (z - q) & (C - 1)
+    return jnp.where(other == q, q >> 2, jnp.where(q < other, 1, 0)) * C
+
+
 def iota(shape, axis):
     return lax.broadcasted_iota(I32, shape, axis)
 
 
-def deal_kernel(ids, off_in, asg_in, res_in, frames_in, out, frames, off, asg, res, shifted, details, count, sems):
+def deal_kernel(off_in, asg_in, res_in, frames_in, out, frames, off, asg, res, shifted, details, count, sems):
     copies = [
         pltpu.make_async_copy(source, target, sems.at[i])
         for i, (source, target) in enumerate(
@@ -80,7 +91,7 @@
     lane, row = iota((8, N), 1), iota((8, N), 0)
     for p in range(PD):
         for k in range(C):
-            c = (asg[p, k] + ids[2]) & (C - 1)
+            c = (asg[p, k] + place()[2]) & (C - 1)
             slot = count[c]
             count[c] = slot + 1
             at = pl.multiple_of(slot * N, N)
@@ -193,7 +204,7 @@
     zero = jnp.zeros((N, N), F32)
     low, high = weighted(moved, w_low, w_high, zero, zero)
     lines = [jnp.broadcast_to(v, (1, N)) for s in (low_sum, high_sum) for v in pieces(s)]
-    tail = jnp.concatenate(lines + [jnp.zeros((10, N), F32)], 0).astype(BF16)
+    tail = jnp.concatenate(lines + [jnp.zeros((2, N), F32)], 0).astype(BF16)
     low, high = low.astype(BF16), high.astype(BF16)
     for b in range(C):
         msg[b, :N, :] = low
@@ -201,9 +212,9 @@
         msg[b, 2 * N :, :] = tail
 
 
-def second_kernel(ids, got, old, spec, moved, phase, info, table, right, left, msg, tables_out, along, w_low, w_high, tiles):
+def second_kernel(got, old, spec, moved, phase, info, table, right, left, msg, tables_out, along, w_low, w_high, tiles):
     total = jnp.zeros((2 * N, N), F32)
-    tail = jnp.zeros((16, N), F32)
+    tail = jnp.zeros((8, N), F32)
     for b in range(C):
         total = total + got[b, : 2 * N, :].astype(F32)
         tail = tail + got[b, 2 * N :, :].astype(F32)
@@ -216,31 +227,34 @@
     match(spec, tiles, info, phase, along)
     scores, low_sum, high_sum = weigh(along, info, w_low, w_high, 1)
     tables_out[...] = table[...] + scores
-    own = jnp.where(ids[0] == 0, 1.0, 0.0)
+    own = jnp.where(place()[0] == 0, 1.0, 0.0)
     low, high = weighted(
         moved, w_low, w_high, fresh[0].astype(F32) * own, fresh[1].astype(F32) * own
     )
-    lines = [jnp.broadcast_to(s + own, (1, N)) for s in (low_sum, high_sum)]
-    tail = jnp.concatenate(lines + [jnp.zeros((6, N), F32)], 0)
+    lines = [
+        jnp.broadcast_to(v, (1, N)) for s in (low_sum, high_sum) for v in pieces(s + own)
+    ]
+    tail = jnp.concatenate(lines + [jnp.zeros((2, N), F32)], 0).astype(BF16)
+    low, high = low.astype(BF16), high.astype(BF16)
     msg[...] = jnp.zeros_like(msg)
+    half = own_half()
     for b in range(C):
-        at = ids[1] * C + b
-        msg[at, :SLAB, :] = low[b * SLAB : (b + 1) * SLAB]
-        msg[at, SLAB : 2 * SLAB, :] = high[b * SLAB : (b + 1) * SLAB]
-        msg[at, 2 * SLAB :, :] = tail
-
-
-def finish_kernel(ids, got, table, msg):
-    total = got[ids[1] * C]
+        msg[half + b, :SLAB, :] = low[b * SLAB : (b + 1) * SLAB]
+        msg[half + b, SLAB : 2 * SLAB, :] = high[b * SLAB : (b + 1) * SLAB]
+        msg[half + b, 2 * SLAB :, :] = tail
+
+
+def finish_kernel(got, table, msg):
+    half = own_half()
+    total = got[half].astype(F32)
     for b in range(1, C):
-        total = total + got[ids[1] * C + b]
-    slab = jnp.concatenate(
-        [
-            total[p * SLAB : (p + 1) * SLAB] / total[2 * SLAB + p : 2 * SLAB + p + 1]
-            for p in range(PD)
-        ],
-        0,
-    ).astype(BF16)
+        total = total + got[half + b].astype(F32)
+    tail = total[2 * SLAB :]
+    slab = []
+    for p in range(PD):
+        count = tail[3 * p : 3 * p + 1] + tail[3 * p + 1 : 3 * p + 2] + tail[3 * p + 2 : 3 * p + 3]
+        slab.append(total[p * SLAB : (p + 1) * SLAB] / count)
+    slab = jnp.concatenate(slab, 0).astype(BF16)
     parts = pieces(table[...])
     pad = jnp.zeros((5, N), F32)
     for v in range(C):
@@ -250,30 +264,39 @@
             msg[y * C + v, 2 * SLAB :, :] = lines
 
 
-def place_kernel(ids, got, out, scores):
-    for y in range(C):
-        for z in range(C):
-            group = (z - ids[2]) & (C - 1)
-            for p in range(PD):
-                out[PD * group + p, y * SLAB : (y + 1) * SLAB, :] = got[
-                    y * C + z, p * SLAB : (p + 1) * SLAB, :
-                ]
+def place_kernel(got, out, scores, sems):
+    y, _, q = place()
+    copies = []
+    for z in range(C):
+        group = (z - q) & (C - 1)
+        for p in range(PD):
+            copies.append(
+                pltpu.make_async_copy(
+                    got.at[:, z, p * SLAB : (p + 1) * SLAB, :],
+                    out.at[PD * group + p],
+                    sems.at[PD * z + p],
+                )
+            )
+    for copy in copies:
+        copy.start()
     total = jnp.zeros((8, N), F32)
     for c in range(C):
-        total = total + got[ids[0] * C + c, 2 * SLAB :, :].astype(F32)
+        total = total + got[y, c, 2 * SLAB :, :].astype(F32)
     line = total[0:1] + total[1:2] + total[2:3]
     for j in range(2 * PD):
         scores[j // PD, 0, j % PD, :, :] = line[:, j * C : (j + 1) * C]
-
-
-def call(kernel, outs, ins, scratch, args, flops=1e8, grant=16):
+    for copy in copies:
+        copy.wait()
+
+
+def call(kernel, outs, ins, scratch, args, flops=1e8, grant=16, spread=None):
     spaces = {"s": pltpu.SMEM, "v": pltpu.VMEM, "h": pltpu.HBM}
     size = sum(int(np.prod(o.shape)) * o.dtype.itemsize for o in outs)
     return pl.pallas_call(
         kernel,
         out_shape=outs,
         in_specs=[pl.BlockSpec(memory_space=spaces[i]) for i in ins],
-        out_specs=[pl.BlockSpec(memory_space=pltpu.VMEM) for _ in outs],
+        out_specs=[pl.BlockSpec(memory_space=spaces[o]) for o in spread or "v" * len(outs)],
         scratch_shapes=scratch,
         compiler_params=pltpu.CompilerParams(vmem_limit_bytes=grant << 20),
         cost_estimate=pl.CostEstimate(
@@ -320,17 +343,13 @@
     off = offsets.reshape(PD, 2)
     asg = assign.reshape(PD, C)
     res = residual.reshape(PD, C, 2).transpose(0, 2, 1)
-    t = lax.axis_index("tm").astype(I32)
-    q = lax.axis_index("plane").astype(I32)
-    y, z = t >> 3, t & 7
+    _, z, q = place()
     other = (z - q) & (C - 1)
-    half = jnp.where(other == q, q >> 2, (q < other).astype(I32))
-    ids = jnp.stack([y, half, q])
     small = (PAIRS, 8, N)
     (dealt,) = call(
         deal_kernel,
         [struct((C, ROWS, N), BF16)],
-        "shhhh",
+        "hhhh",
         [
             pltpu.VMEM((PD, N, C * N), BF16),
             pltpu.SMEM((PD, 2), I32),
@@ -341,7 +360,7 @@
             pltpu.SMEM((C,), I32),
             pltpu.SemaphoreType.DMA((4,)),
         ],
-        (ids, off, asg, res, frames[0]),
+        (off, asg, res, frames[0]),
         grant=63,
     )
     got = exchange(dealt, "tm", along_z())
@@ -358,7 +377,7 @@
     msg, spec, moved, phase, info, table = call(
         first_kernel,
         [
-            struct((C, 2 * N + 16, N), BF16),
+            struct((C, 2 * N + 8, N), BF16),
             struct((PAIRS, 2 * N, 2 * N), F32),
             struct((2 * PAIRS, N, N), BF16),
             struct(small, F32),
@@ -373,25 +392,24 @@
     got = exchange(msg, "tm", along_y())
     msg, table = call(
         second_kernel,
-        [struct((2 * C, 2 * SLAB + 8, N), F32), struct((C, N), F32)],
-        "svvvvvvvvv",
+        [struct((2 * C, 2 * SLAB + 8, N), BF16), struct((C, N), F32)],
+        "vvvvvvvvv",
         scratch + [pltpu.VMEM((2 * N, 2 * N), F32)],
-        (ids, got, old, spec, moved, phase, info, table, right, left),
+        (got, old, spec, moved, phase, info, table, right, left),
         flops=1e9,
     )
     got = exchange(msg, ("tm", "plane"), across())
-    (msg,) = call(
-        finish_kernel, [struct((C * C, 2 * SLAB + 8, N), BF16)], "svv", [], (ids, got, table)
-    )
+    (msg,) = call(finish_kernel, [struct((C * C, 2 * SLAB + 8, N), BF16)], "vv", [], (got, table))
     got = exchange(msg, "tm")
     out, scores = call(
         place_kernel,
-        [struct((PD * C, N, N), BF16), struct((2, 1, PD, 1, C), F32)],
-        "sv",
-        [],
-        (ids, got),
-    )
-    return out, scores
+        [struct((PD * C, C, SLAB, N), BF16), struct((2, 1, PD, 1, C), F32)],
+        "v",
+        [pltpu.SemaphoreType.DMA((PD * C,))],
+        (got.reshape(C, C, 2 * SLAB + 8, N),),
+        spread="hv",
+    )
+    return out.reshape(PD * C, N, N), scores
 
 
 def solution(mesh):

time: 125 us -> 119 us (0.952)
  blocking collectives: 68.4 us -> 64.9 us
  Pallas kernels: 15.5 us -> 13.8 us
    all_to_all x3, blocking collectives: 68.4 us -> 64.9 us  [exchange(): lax.all_to_all(value, axis, split_axis=0, concat_axis=0, axis_index_group...]
    pallas_call x6, Pallas kernels: 15.5 us -> 13.8 us  [call(): pl.pallas_call(kernel, out_shape=outs, in_specs=[pl.BlockSpec(memory_spac...]
where the time goes in v5:
time: 119 us
  blocking collectives  64.9 us (55%)
  waiting for transfers between devices  28.3 us (24%)
  Pallas kernels  13.8 us (12%)
  starting transfers between devices  11.1 us (9%)
    all_to_all x3, blocking collectives, exchange(): lax.all_to_all(value, axis, split_axis=0, concat_axis=0, axis_index_group...  64.9 us
    all_to_all x1, waiting for transfers between devices, exchange(): lax.all_to_all(value, axis, split_axis=0, concat_axis=0, axis_index_group...  28.3 us
    pallas_call x6, Pallas kernels, call(): pl.pallas_call(kernel, out_shape=outs, in_specs=[pl.BlockSpec(memory_spac...  13.8 us
    all_to_all x1, starting transfers between devices, exchange(): lax.all_to_all(value, axis, split_axis=0, concat_axis=0, axis_index_group...  10.5 us
  transfers between devices with their start and end apart: 2, of which 1 were waited for; matrix products, arithmetic and copies ran while one was open for 0% of the time, Pallas kernels for 0%

profile of v5, /device:TPU:16, one launch (start us, length us, event | category | flops | bytes accessed | tf_op | source)
XLA Modules:
  0.0 118.9 jit_solution(15991241660987117128)
XLA Ops:
  0.6 0.0 copy-start
  0.6 2.7 %shard_map.95 = bf16[8,528,128]{2,1,0:T(8,128)(2,1)} custom-call(s32[2,2]{1,0:T(2,128)} %bitcast.13, s32[2,8]{1,0:T(2,128)} %bitcast.14, s32[2,2,8]{2,1,0:T(2,128)} %bitcast.12, bf16[2,128,1024]{2,1,0:T(8,128)(2,1)} %bitcast.10), custom_call_target="tpu_custom_call" | custom-call | flops 100000000 | bytes 2129920 | tf_op jit(solution)/shard_map/pallas_call | solution.py:295
  3.4 0.0 copy-start.1
  3.4 0.0 copy-start.2
  3.4 0.0 copy-start.3
  3.4 10.5 %all-to-all-start = ((bf16[8,528,128]{2,1,0:T(8,128)(2,1)}), bf16[8,528,128]{2,1,0:T(8,128)(2,1)S(1)}, u32[]{:S(2)}, u32[]{:S(2)}) async-start(bf16[8,528,128]{2,1,0:T(8,128)(2,1)} %shard_map.95), calls=%async_computation | async-start | bytes 2162688 | tf_op jit(solution)/shard_map/all_to_all | solution.py:336
  13.9 0.0 copy-done
  13.9 0.7 collective-permute-start
  14.6 0.0 collective-permute-done.pair.old
  14.6 0.0 copy-done.1
  14.6 0.0 copy-done.2
  14.6 0.4 shard_map.96.tiles
  15.0 28.3 %all-to-all-done.got = bf16[8,528,128]{2,1,0:T(8,128)(2,1)S(1)} async-done(((bf16[8,528,128]{2,1,0:T(8,128)(2,1)}), bf16[8,528,128]{2,1,0:T(8,128)(2,1)S(1)}, u32[]{:S(2)}, u32[]{:S(2)}) %all-to-all-start) | async-done | bytes 1081376 | tf_op jit(solution)/shard_map/all_to_all | solution.py:336
  43.3 0.0 copy-done.3
  43.3 5.5 %shard_map.97 = (bf16[8,264,128]{2,1,0:T(8,128)(2,1)S(1)}, f32[16,256,256]{2,1,0:T(8,128)S(1)}, bf16[32,128,128]{2,1,0:T(8,128)(2,1)S(1)}, f32[16,8,128]{2,1,0:T...) custom-call(bf16[8,528,128]{2,1,0:T(8,128)(2,1)S(1)} %all-to-all-done.got, f32[256,256]{1,0:T(8,128)S(1)} %shard_map.96.tiles, ...), custom_call_target="tpu_custom_call" | custom-call | flops 1000000000 | bytes 6967296 | tf_op jit(solution)/shard_map/pallas_call | solution.py:295
  48.8 22.9 %all_to_all.20.got = bf16[8,264,128]{2,1,0:T(8,128)(2,1)S(1)} all-to-all(bf16[8,264,128]{2,1,0:T(8,128)(2,1)S(1)} %get-tuple-element.12), channel_id=1, replica_groups={{0,64,128,192,256,320,384,448},{8,72,136,200,264,328,392,456},{16,80,14..., dimensions={0} | all-to-all | bytes 1081344 | tf_op jit(solution)/shard_map/all_to_all | solution.py:336
  71.7 3.6 %shard_map.98 = (bf16[16,40,128]{2,1,0:T(8,128)(2,1)S(1)}, f32[8,128]{1,0:T(8,128)S(1)}) custom-call(bf16[8,264,128]{2,1,0:T(8,128)(2,1)S(1)} %all_to_all.20.got, bf16[256,128]{1,0:T(8,128)(2,1)S(1)} %collective-permute-done.pair.old, f32[16,256,256]{2,1,0:T(8,128)S(1)} %get-tuple-element.13.spec, bf16[32,128,128]{2,1,0:T(8,128)(2,1)S(1)} %get-tuple-element.14.moved, ...), custom_call_target="tpu_custom_call" | custom-call | flops 1000000000 | bytes 1216512 | tf_op jit(solution)/shard_map/pallas_call | solution.py:295
  75.3 15.3 %all_to_all.21.got = bf16[16,40,128]{2,1,0:T(8,128)(2,1)S(1)} all-to-all(bf16[16,40,128]{2,1,0:T(8,128)(2,1)S(1)} %get-tuple-element.18), channel_id=1, replica_groups={{1,65,129,193,257,321,385,449,7,71,135,199,263,327,391,455},{2,66,130,1..., dimensions={0} | all-to-all | bytes 327680 | tf_op jit(solution)/shard_map/all_to_all | solution.py:336
  90.6 0.1 shard_map.99
  90.7 26.7 %all_to_all.22 = bf16[64,40,128]{2,1,0:T(8,128)(2,1)S(1)} all-to-all(bf16[64,40,128]{2,1,0:T(8,128)(2,1)S(1)} %shard_map.99), channel_id=1, replica_groups=mesh['tm'=64,'plane'=8] {'tm'}, dimensions={0} | all-to-all | bytes 1310720 | tf_op jit(solution)/shard_map/all_to_all | solution.py:336
  117.4 1.5 %shard_map.100 = (bf16[16,8,16,128]{3,2,1,0:T(8,128)(2,1)}, f32[2,1,2,1,8]{4,3,2,1,0:T(1,128)}) custom-call(bf16[8,8,40,128]{3,2,1,0:T(8,128)(2,1)S(1)} %bitcast.9), custom_call_target="tpu_custom_call" | custom-call | flops 100000000 | bytes 1572992 | tf_op jit(solution)/shard_map/pallas_call | solution.py:295
  (1 shorter events, 0.0 us)
Async XLA Ops:
  0.6 13.3 %copy-start = (bf16[16,128,128]{2,1,0:T(8,128)(2,1)S(1)}, bf16[16,128,128]{2,1,0:T(8,128)(2,1)}, u32[]{:S(2)}) copy-start(bf16[16,128,128]{2,1,0:T(8,128)(2,1)} %param.12) | copy-start | bytes 1572868
  3.4 11.2 %copy-start.1 = (bf16[256,256]{1,0:T(8,128)(2,1)S(1)}, bf16[256,256]{1,0:T(8,128)(2,1)}, u32[]{:S(2)}) copy-start(bf16[256,256]{1,0:T(8,128)(2,1)} %constant.24.clone.left) | copy-start | bytes 393220
  3.4 11.2 %copy-start.2 = (bf16[128,256]{1,0:T(8,128)(2,1)S(1)}, bf16[128,256]{1,0:T(8,128)(2,1)}, u32[]{:S(2)}) copy-start(bf16[128,256]{1,0:T(8,128)(2,1)} %constant.23.clone.right) | copy-start | bytes 196612
  3.4 39.9 %copy-start.3 = (bf16[128,256]{1,0:T(8,128)(2,1)S(1)}, bf16[128,256]{1,0:T(8,128)(2,1)}, u32[]{:S(2)}) copy-start(bf16[128,256]{1,0:T(8,128)(2,1)} %constant.25.clone.rows) | copy-start | bytes 196612
  3.4 39.9 %all-to-all-start = ((bf16[8,528,128]{2,1,0:T(8,128)(2,1)}), bf16[8,528,128]{2,1,0:T(8,128)(2,1)S(1)}, u32[]{:S(2)}, u32[]{:S(2)}) async-start(bf16[8,528,128]{2,1,0:T(8,128)(2,1)} %shard_map.95), calls=%async_computation | async-start | bytes 2162688 | tf_op jit(solution)/shard_map/all_to_all | solution.py:336
  13.9 0.7 collective-permute-start

commit v6 on v5

--- a/solution.py
+++ b/solution.py
@@ -144,7 +144,7 @@
         along[i, 0:2, :] = along_of(spec[i], tiles[...], info[i], phase[i])
         return carry
 
-    lax.fori_loop(0, PAIRS, one, 0, unroll=8)
+    lax.fori_loop(0, PAIRS, one, 0, unroll=16)
 
 
 def weigh(along, info, w_low, w_high, turn):
@@ -173,7 +173,7 @@
             high = high + patch * wh[e : e + 1]
         return low, high
 
-    return lax.fori_loop(0, PAIRS, one, (low, high), unroll=2)
+    return lax.fori_loop(0, PAIRS, one, (low, high), unroll=16)
 
 
 def first_kernel(got, tiles, right, left, rows, msg, spec, moved, phase, info, table, along, w_low, w_high):
@@ -197,7 +197,7 @@
             moved[2 * i + e] = pltpu.roll(patch, across, 1).astype(BF16)
         return carry
 
-    lax.fori_loop(0, PAIRS, one, 0, unroll=8)
+    lax.fori_loop(0, PAIRS, one, 0, unroll=16)
     match(spec, tiles, info, phase, along)
     scores, low_sum, high_sum = weigh(along, info, w_low, w_high, 0)
     table[...] = scores

time: 119 us -> 118 us (level)
  Pallas kernels: 13.8 us -> 12.1 us
    pallas_call x6, Pallas kernels: 13.8 us -> 12.1 us  [call(): pl.pallas_call(kernel, out_shape=outs, in_specs=[pl.BlockSpec(memory_spac...]
where the time goes in v6:
time: 118 us; the launch traced here: 117 us
  blocking collectives  64.9 us (55%)
  waiting for transfers between devices  28.3 us (24%)
  Pallas kernels  12.1 us (10%)
  starting transfers between devices  11.1 us (9%)
    all_to_all x3, blocking collectives, exchange(): lax.all_to_all(value, axis, split_axis=0, concat_axis=0, axis_index_group...  64.9 us
    all_to_all x1, waiting for transfers between devices, exchange(): lax.all_to_all(value, axis, split_axis=0, concat_axis=0, axis_index_group...  28.3 us
    pallas_call x6, Pallas kernels, call(): pl.pallas_call(kernel, out_shape=outs, in_specs=[pl.BlockSpec(memory_spac...  12.1 us
    all_to_all x1, starting transfers between devices, exchange(): lax.all_to_all(value, axis, split_axis=0, concat_axis=0, axis_index_group...  10.5 us
  transfers between devices with their start and end apart: 2, of which 1 were waited for; matrix products, arithmetic and copies ran while one was open for 0% of the time, Pallas kernels for 0%

profile of v6, /device:TPU:16, one launch (start us, length us, event | category | flops | bytes accessed | tf_op | source)
XLA Modules:
  0.0 117.3 jit_solution(2334942199096650810)
XLA Ops:
  0.6 0.0 copy-start
  0.6 2.7 %shard_map.95 = bf16[8,528,128]{2,1,0:T(8,128)(2,1)} custom-call(s32[2,2]{1,0:T(2,128)} %bitcast.13, s32[2,8]{1,0:T(2,128)} %bitcast.14, s32[2,2,8]{2,1,0:T(2,128)} %bitcast.12, bf16[2,128,1024]{2,1,0:T(8,128)(2,1)} %bitcast.10), custom_call_target="tpu_custom_call" | custom-call | flops 100000000 | bytes 2129920 | tf_op jit(solution)/shard_map/pallas_call | solution.py:295
  3.4 0.0 copy-start.1
  3.4 0.0 copy-start.2
  3.4 0.0 copy-start.3
  3.4 10.5 %all-to-all-start = ((bf16[8,528,128]{2,1,0:T(8,128)(2,1)}), bf16[8,528,128]{2,1,0:T(8,128)(2,1)S(1)}, u32[]{:S(2)}, u32[]{:S(2)}) async-start(bf16[8,528,128]{2,1,0:T(8,128)(2,1)} %shard_map.95), calls=%async_computation | async-start | bytes 2162688 | tf_op jit(solution)/shard_map/all_to_all | solution.py:336
  13.9 0.0 copy-done
  13.9 0.7 collective-permute-start
  14.6 0.0 collective-permute-done.pair.old
  14.6 0.0 copy-done.1
  14.6 0.0 copy-done.2
  14.6 0.4 shard_map.96.tiles
  15.0 28.3 %all-to-all-done.got = bf16[8,528,128]{2,1,0:T(8,128)(2,1)S(1)} async-done(((bf16[8,528,128]{2,1,0:T(8,128)(2,1)}), bf16[8,528,128]{2,1,0:T(8,128)(2,1)S(1)}, u32[]{:S(2)}, u32[]{:S(2)}) %all-to-all-start) | async-done | bytes 1081376 | tf_op jit(solution)/shard_map/all_to_all | solution.py:336
  43.3 0.0 copy-done.3
  43.3 4.2 %shard_map.97 = (bf16[8,264,128]{2,1,0:T(8,128)(2,1)S(1)}, f32[16,256,256]{2,1,0:T(8,128)S(1)}, bf16[32,128,128]{2,1,0:T(8,128)(2,1)S(1)}, f32[16,8,128]{2,1,0:T...) custom-call(bf16[8,528,128]{2,1,0:T(8,128)(2,1)S(1)} %all-to-all-done.got, f32[256,256]{1,0:T(8,128)S(1)} %shard_map.96.tiles, ...), custom_call_target="tpu_custom_call" | custom-call | flops 1000000000 | bytes 6967296 | tf_op jit(solution)/shard_map/pallas_call | solution.py:295
  47.6 22.9 %all_to_all.20.got = bf16[8,264,128]{2,1,0:T(8,128)(2,1)S(1)} all-to-all(bf16[8,264,128]{2,1,0:T(8,128)(2,1)S(1)} %get-tuple-element.12), channel_id=1, replica_groups={{0,64,128,192,256,320,384,448},{8,72,136,200,264,328,392,456},{16,80,14..., dimensions={0} | all-to-all | bytes 1081344 | tf_op jit(solution)/shard_map/all_to_all | solution.py:336
  70.4 3.2 %shard_map.98 = (bf16[16,40,128]{2,1,0:T(8,128)(2,1)S(1)}, f32[8,128]{1,0:T(8,128)S(1)}) custom-call(bf16[8,264,128]{2,1,0:T(8,128)(2,1)S(1)} %all_to_all.20.got, bf16[256,128]{1,0:T(8,128)(2,1)S(1)} %collective-permute-done.pair.old, f32[16,256,256]{2,1,0:T(8,128)S(1)} %get-tuple-element.13.spec, bf16[32,128,128]{2,1,0:T(8,128)(2,1)S(1)} %get-tuple-element.14.moved, ...), custom_call_target="tpu_custom_call" | custom-call | flops 1000000000 | bytes 1216512 | tf_op jit(solution)/shard_map/pallas_call | solution.py:295
  73.6 15.3 %all_to_all.21.got = bf16[16,40,128]{2,1,0:T(8,128)(2,1)S(1)} all-to-all(bf16[16,40,128]{2,1,0:T(8,128)(2,1)S(1)} %get-tuple-element.18), channel_id=1, replica_groups={{1,65,129,193,257,321,385,449,7,71,135,199,263,327,391,455},{2,66,130,1..., dimensions={0} | all-to-all | bytes 327680 | tf_op jit(solution)/shard_map/all_to_all | solution.py:336
  88.9 0.1 shard_map.99
  89.0 26.7 %all_to_all.22 = bf16[64,40,128]{2,1,0:T(8,128)(2,1)S(1)} all-to-all(bf16[64,40,128]{2,1,0:T(8,128)(2,1)S(1)} %shard_map.99), channel_id=1, replica_groups=mesh['tm'=64,'plane'=8] {'tm'}, dimensions={0} | all-to-all | bytes 1310720 | tf_op jit(solution)/shard_map/all_to_all | solution.py:336
  115.8 1.5 %shard_map.100 = (bf16[16,8,16,128]{3,2,1,0:T(8,128)(2,1)}, f32[2,1,2,1,8]{4,3,2,1,0:T(1,128)}) custom-call(bf16[8,8,40,128]{3,2,1,0:T(8,128)(2,1)S(1)} %bitcast.9), custom_call_target="tpu_custom_call" | custom-call | flops 100000000 | bytes 1572992 | tf_op jit(solution)/shard_map/pallas_call | solution.py:295
  (1 shorter events, 0.0 us)
Async XLA Ops:
  0.6 13.3 %copy-start = (bf16[16,128,128]{2,1,0:T(8,128)(2,1)S(1)}, bf16[16,128,128]{2,1,0:T(8,128)(2,1)}, u32[]{:S(2)}) copy-start(bf16[16,128,128]{2,1,0:T(8,128)(2,1)} %param.12) | copy-start | bytes 1572868
  3.4 11.2 %copy-start.1 = (bf16[256,256]{1,0:T(8,128)(2,1)S(1)}, bf16[256,256]{1,0:T(8,128)(2,1)}, u32[]{:S(2)}) copy-start(bf16[256,256]{1,0:T(8,128)(2,1)} %constant.24.clone.left) | copy-start | bytes 393220
  3.4 11.2 %copy-start.2 = (bf16[128,256]{1,0:T(8,128)(2,1)S(1)}, bf16[128,256]{1,0:T(8,128)(2,1)}, u32[]{:S(2)}) copy-start(bf16[128,256]{1,0:T(8,128)(2,1)} %constant.23.clone.right) | copy-start | bytes 196612
  3.4 39.9 %copy-start.3 = (bf16[128,256]{1,0:T(8,128)(2,1)S(1)}, bf16[128,256]{1,0:T(8,128)(2,1)}, u32[]{:S(2)}) copy-start(bf16[128,256]{1,0:T(8,128)(2,1)} %constant.25.clone.rows) | copy-start | bytes 196612
  3.4 39.9 %all-to-all-start = ((bf16[8,528,128]{2,1,0:T(8,128)(2,1)}), bf16[8,528,128]{2,1,0:T(8,128)(2,1)S(1)}, u32[]{:S(2)}, u32[]{:S(2)}) async-start(bf16[8,528,128]{2,1,0:T(8,128)(2,1)} %shard_map.95), calls=%async_computation | async-start | bytes 2162688 | tf_op jit(solution)/shard_map/all_to_all | solution.py:336
  13.9 0.7 collective-permute-start

commit v7 on v6

--- a/solution.py
+++ b/solution.py
@@ -72,7 +72,13 @@
     copies = [
         pltpu.make_async_copy(source, target, sems.at[i])
         for i, (source, target) in enumerate(
-            ((off_in, off), (asg_in, asg), (res_in, res), (frames_in, frames))
+            (
+                (off_in, off),
+                (asg_in, asg),
+                (res_in, res),
+                (frames_in.at[0], frames.at[0]),
+                (frames_in.at[1], frames.at[1]),
+            )
         )
     ]
     for copy in copies:
@@ -81,9 +87,10 @@
     details[...] = jnp.zeros_like(details)
     for c in range(C):
         count[c] = 0
-    for copy in copies:
+    for copy in copies[:3]:
         copy.wait()
     for p in range(PD):
+        copies[3 + p].wait()
         plane = frames[p].astype(F32)
         plane = pltpu.roll(plane, (-off[p, 0]) & (N - 1), 0)
         plane = pltpu.roll(plane, (-off[p, 1]) & (C * N - 1), 1)
@@ -125,7 +132,7 @@
         c_im = p_im * t_re - p_re * t_im
         modulus = jnp.sqrt(c_re * c_re + c_im * c_im)
         level = jnp.sum(jnp.sum(modulus, 0, keepdims=True), 1, keepdims=True) * (1.0 / (N * N))
-        scale = 1.0 / (modulus + 0.1 * level + 1e-06)
+        scale = 1.0 / (modulus + (0.1 * level + 1e-06))
         n_re = (c_re * scale).astype(BF16)
         n_im = (c_im * scale).astype(BF16)
         lhs = jnp.concatenate([phase[e : e + 1], phase[2 + e : 3 + e]], 0).astype(BF16)
@@ -264,21 +271,17 @@
             msg[y * C + v, 2 * SLAB :, :] = lines
 
 
-def place_kernel(got, out, scores, sems):
+def place_kernel(got, out, scores, tiles, sems):
     y, _, q = place()
     copies = []
     for z in range(C):
         group = (z - q) & (C - 1)
-        for p in range(PD):
-            copies.append(
-                pltpu.make_async_copy(
-                    got.at[:, z, p * SLAB : (p + 1) * SLAB, :],
-                    out.at[PD * group + p],
-                    sems.at[PD * z + p],
-                )
-            )
-    for copy in copies:
+        for b in range(C):
+            for p in range(PD):
+                tiles[z, p, b] = got[b, z, p * SLAB : (p + 1) * SLAB, :]
+        copy = pltpu.make_async_copy(tiles.at[z], out.at[group], sems.at[z])
         copy.start()
+        copies.append(copy)
     total = jnp.zeros((8, N), F32)
     for c in range(C):
         total = total + got[y, c, 2 * SLAB :, :].astype(F32)
@@ -358,7 +361,7 @@
             pltpu.VMEM((PD, N, C * N), BF16),
             pltpu.VMEM((C * CAP // 2, 8, N), F32),
             pltpu.SMEM((C,), I32),
-            pltpu.SemaphoreType.DMA((4,)),
+            pltpu.SemaphoreType.DMA((5,)),
         ],
         (off, asg, res, frames[0]),
         grant=63,
@@ -403,9 +406,9 @@
     got = exchange(msg, "tm")
     out, scores = call(
         place_kernel,
-        [struct((PD * C, C, SLAB, N), BF16), struct((2, 1, PD, 1, C), F32)],
+        [struct((C, PD, C, SLAB, N), BF16), struct((2, 1, PD, 1, C), F32)],
         "v",
-        [pltpu.SemaphoreType.DMA((PD * C,))],
+        [pltpu.VMEM((C, PD, C, SLAB, N), BF16), pltpu.SemaphoreType.DMA((C,))],
         (got.reshape(C, C, 2 * SLAB + 8, N),),
         spread="hv",
     )

time: 118 us -> 117 us (level)
  no operation moved by 1% of the time
where the time goes in v7:
time: 117 us
  blocking collectives  64.9 us (55%)
  waiting for transfers between devices  28.3 us (24%)
  Pallas kernels  12 us (10%)
  starting transfers between devices  11.1 us (9%)
    all_to_all x3, blocking collectives, exchange(): lax.all_to_all(value, axis, split_axis=0, concat_axis=0, axis_index_group...  64.9 us
    all_to_all x1, waiting for transfers between devices, exchange(): lax.all_to_all(value, axis, split_axis=0, concat_axis=0, axis_index_group...  28.3 us
    pallas_call x6, Pallas kernels, call(): pl.pallas_call(kernel, out_shape=outs, in_specs=[pl.BlockSpec(memory_spac...  12 us
    all_to_all x1, starting transfers between devices, exchange(): lax.all_to_all(value, axis, split_axis=0, concat_axis=0, axis_index_group...  10.5 us
  transfers between devices with their start and end apart: 2, of which 1 were waited for; matrix products, arithmetic and copies ran while one was open for 0% of the time, Pallas kernels for 0%

profile of v7, /device:TPU:16, one launch (start us, length us, event | category | flops | bytes accessed | tf_op | source)
XLA Modules:
  0.0 117.1 jit_solution(5588907488737983922)
XLA Ops:
  0.6 0.0 copy-start
  0.6 2.6 %shard_map.95 = bf16[8,528,128]{2,1,0:T(8,128)(2,1)} custom-call(s32[2,2]{1,0:T(2,128)} %bitcast.13, s32[2,8]{1,0:T(2,128)} %bitcast.14, s32[2,2,8]{2,1,0:T(2,128)} %bitcast.12, bf16[2,128,1024]{2,1,0:T(8,128)(2,1)} %bitcast.10), custom_call_target="tpu_custom_call" | custom-call | flops 100000000 | bytes 2129920 | tf_op jit(solution)/shard_map/pallas_call | solution.py:298
  3.3 0.0 copy-start.1
  3.3 0.0 copy-start.2
  3.3 0.0 copy-start.3
  3.3 10.5 %all-to-all-start = ((bf16[8,528,128]{2,1,0:T(8,128)(2,1)}), bf16[8,528,128]{2,1,0:T(8,128)(2,1)S(1)}, u32[]{:S(2)}, u32[]{:S(2)}) async-start(bf16[8,528,128]{2,1,0:T(8,128)(2,1)} %shard_map.95), calls=%async_computation | async-start | bytes 2162688 | tf_op jit(solution)/shard_map/all_to_all | solution.py:339
  13.8 0.0 copy-done
  13.8 0.7 collective-permute-start
  14.5 0.0 collective-permute-done.pair.old
  14.5 0.0 copy-done.1
  14.5 0.0 copy-done.2
  14.5 0.4 shard_map.96.tiles
  14.9 28.3 %all-to-all-done.got = bf16[8,528,128]{2,1,0:T(8,128)(2,1)S(1)} async-done(((bf16[8,528,128]{2,1,0:T(8,128)(2,1)}), bf16[8,528,128]{2,1,0:T(8,128)(2,1)S(1)}, u32[]{:S(2)}, u32[]{:S(2)}) %all-to-all-start) | async-done | bytes 1081376 | tf_op jit(solution)/shard_map/all_to_all | solution.py:339
  43.2 0.0 copy-done.3
  43.2 4.2 %shard_map.97 = (bf16[8,264,128]{2,1,0:T(8,128)(2,1)S(1)}, f32[16,256,256]{2,1,0:T(8,128)S(1)}, bf16[32,128,128]{2,1,0:T(8,128)(2,1)S(1)}, f32[16,8,128]{2,1,0:T...) custom-call(bf16[8,528,128]{2,1,0:T(8,128)(2,1)S(1)} %all-to-all-done.got, f32[256,256]{1,0:T(8,128)S(1)} %shard_map.96.tiles, ...), custom_call_target="tpu_custom_call" | custom-call | flops 1000000000 | bytes 6967296 | tf_op jit(solution)/shard_map/pallas_call | solution.py:298
  47.4 22.9 %all_to_all.20.got = bf16[8,264,128]{2,1,0:T(8,128)(2,1)S(1)} all-to-all(bf16[8,264,128]{2,1,0:T(8,128)(2,1)S(1)} %get-tuple-element.12), channel_id=1, replica_groups={{0,64,128,192,256,320,384,448},{8,72,136,200,264,328,392,456},{16,80,14..., dimensions={0} | all-to-all | bytes 1081344 | tf_op jit(solution)/shard_map/all_to_all | solution.py:339
  70.3 3.2 %shard_map.98 = (bf16[16,40,128]{2,1,0:T(8,128)(2,1)S(1)}, f32[8,128]{1,0:T(8,128)S(1)}) custom-call(bf16[8,264,128]{2,1,0:T(8,128)(2,1)S(1)} %all_to_all.20.got, bf16[256,128]{1,0:T(8,128)(2,1)S(1)} %collective-permute-done.pair.old, f32[16,256,256]{2,1,0:T(8,128)S(1)} %get-tuple-element.13.spec, bf16[32,128,128]{2,1,0:T(8,128)(2,1)S(1)} %get-tuple-element.14.moved, ...), custom_call_target="tpu_custom_call" | custom-call | flops 1000000000 | bytes 1216512 | tf_op jit(solution)/shard_map/pallas_call | solution.py:298
  73.5 15.3 %all_to_all.21.got = bf16[16,40,128]{2,1,0:T(8,128)(2,1)S(1)} all-to-all(bf16[16,40,128]{2,1,0:T(8,128)(2,1)S(1)} %get-tuple-element.18), channel_id=1, replica_groups={{1,65,129,193,257,321,385,449,7,71,135,199,263,327,391,455},{2,66,130,1..., dimensions={0} | all-to-all | bytes 327680 | tf_op jit(solution)/shard_map/all_to_all | solution.py:339
  88.9 0.1 shard_map.99
  89.0 26.7 %all_to_all.22 = bf16[64,40,128]{2,1,0:T(8,128)(2,1)S(1)} all-to-all(bf16[64,40,128]{2,1,0:T(8,128)(2,1)S(1)} %shard_map.99), channel_id=1, replica_groups=mesh['tm'=64,'plane'=8] {'tm'}, dimensions={0} | all-to-all | bytes 1310720 | tf_op jit(solution)/shard_map/all_to_all | solution.py:339
  115.7 1.4 %shard_map.100 = (bf16[8,2,8,16,128]{4,3,2,1,0:T(8,128)(2,1)}, f32[2,1,2,1,8]{4,3,2,1,0:T(1,128)}) custom-call(bf16[8,8,40,128]{3,2,1,0:T(8,128)(2,1)S(1)} %bitcast.9), custom_call_target="tpu_custom_call" | custom-call | flops 100000000 | bytes 1572992 | tf_op jit(solution)/shard_map/pallas_call | solution.py:298
  (1 shorter events, 0.0 us)
Async XLA Ops:
  0.6 13.2 %copy-start = (bf16[16,128,128]{2,1,0:T(8,128)(2,1)S(1)}, bf16[16,128,128]{2,1,0:T(8,128)(2,1)}, u32[]{:S(2)}) copy-start(bf16[16,128,128]{2,1,0:T(8,128)(2,1)} %param.12) | copy-start | bytes 1572868
  3.3 11.2 %copy-start.1 = (bf16[256,256]{1,0:T(8,128)(2,1)S(1)}, bf16[256,256]{1,0:T(8,128)(2,1)}, u32[]{:S(2)}) copy-start(bf16[256,256]{1,0:T(8,128)(2,1)} %constant.24.clone.left) | copy-start | bytes 393220
  3.3 11.2 %copy-start.2 = (bf16[128,256]{1,0:T(8,128)(2,1)S(1)}, bf16[128,256]{1,0:T(8,128)(2,1)}, u32[]{:S(2)}) copy-start(bf16[128,256]{1,0:T(8,128)(2,1)} %constant.23.clone.right) | copy-start | bytes 196612
  3.3 39.9 %copy-start.3 = (bf16[128,256]{1,0:T(8,128)(2,1)S(1)}, bf16[128,256]{1,0:T(8,128)(2,1)}, u32[]{:S(2)}) copy-start(bf16[128,256]{1,0:T(8,128)(2,1)} %constant.25.clone.rows) | copy-start | bytes 196612
  3.3 39.9 %all-to-all-start = ((bf16[8,528,128]{2,1,0:T(8,128)(2,1)}), bf16[8,528,128]{2,1,0:T(8,128)(2,1)S(1)}, u32[]{:S(2)}, u32[]{:S(2)}) async-start(bf16[8,528,128]{2,1,0:T(8,128)(2,1)} %shard_map.95), calls=%async_computation | async-start | bytes 2162688 | tf_op jit(solution)/shard_map/all_to_all | solution.py:339
  13.8 0.7 collective-permute-start

commit v8 on v6

--- a/solution.py
+++ b/solution.py
@@ -231,11 +231,8 @@
     low, high = weighted(
         moved, w_low, w_high, fresh[0].astype(F32) * own, fresh[1].astype(F32) * own
     )
-    lines = [
-        jnp.broadcast_to(v, (1, N)) for s in (low_sum, high_sum) for v in pieces(s + own)
-    ]
-    tail = jnp.concatenate(lines + [jnp.zeros((2, N), F32)], 0).astype(BF16)
-    low, high = low.astype(BF16), high.astype(BF16)
+    lines = [jnp.broadcast_to(s + own, (1, N)) for s in (low_sum, high_sum)]
+    tail = jnp.concatenate(lines + [jnp.zeros((6, N), F32)], 0)
     msg[...] = jnp.zeros_like(msg)
     half = own_half()
     for b in range(C):
@@ -246,13 +243,12 @@
 
 def finish_kernel(got, table, msg):
     half = own_half()
-    total = got[half].astype(F32)
+    total = got[half]
     for b in range(1, C):
-        total = total + got[half + b].astype(F32)
-    tail = total[2 * SLAB :]
+        total = total + got[half + b]
     slab = []
     for p in range(PD):
-        count = tail[3 * p : 3 * p + 1] + tail[3 * p + 1 : 3 * p + 2] + tail[3 * p + 2 : 3 * p + 3]
+        count = total[2 * SLAB + p : 2 * SLAB + p + 1]
         slab.append(total[p * SLAB : (p + 1) * SLAB] / count)
     slab = jnp.concatenate(slab, 0).astype(BF16)
     parts = pieces(table[...])
@@ -392,7 +388,7 @@
     got = exchange(msg, "tm", along_y())
     msg, table = call(
         second_kernel,
-        [struct((2 * C, 2 * SLAB + 8, N), BF16), struct((C, N), F32)],
+        [struct((2 * C, 2 * SLAB + 8, N), F32), struct((C, N), F32)],
         "vvvvvvvvv",
         scratch + [pltpu.VMEM((2 * N, 2 * N), F32)],
         (got, old, spec, moved, phase, info, table, right, left),

time: 118 us -> 121 us (1.025)
  blocking collectives: 64.9 us -> 68.1 us
    all_to_all x3, blocking collectives: 64.9 us -> 68.1 us  [exchange(): lax.all_to_all(value, axis, split_axis=0, concat_axis=0, axis_index_group...]
where the time goes in v8:
time: 121 us; the launch traced here: 120 us
  blocking collectives  68.1 us (56%)
  waiting for transfers between devices  28.3 us (23%)
  Pallas kernels  12.1 us (10%)
  starting transfers between devices  11.1 us (9%)
    all_to_all x3, blocking collectives, exchange(): lax.all_to_all(value, axis, split_axis=0, concat_axis=0, axis_index_group...  68.1 us
    all_to_all x1, waiting for transfers between devices, exchange(): lax.all_to_all(value, axis, split_axis=0, concat_axis=0, axis_index_group...  28.3 us
    pallas_call x6, Pallas kernels, call(): pl.pallas_call(kernel, out_shape=outs, in_specs=[pl.BlockSpec(memory_spac...  12.1 us
    all_to_all x1, starting transfers between devices, exchange(): lax.all_to_all(value, axis, split_axis=0, concat_axis=0, axis_index_group...  10.5 us
  transfers between devices with their start and end apart: 2, of which 1 were waited for; matrix products, arithmetic and copies ran while one was open for 0% of the time, Pallas kernels for 0%

profile of v8, /device:TPU:16, one launch (start us, length us, event | category | flops | bytes accessed | tf_op | source)
XLA Modules:
  0.0 120.4 jit_solution(1097326369398414255)
XLA Ops:
  0.6 0.0 copy-start
  0.6 2.7 %shard_map.95 = bf16[8,528,128]{2,1,0:T(8,128)(2,1)} custom-call(s32[2,2]{1,0:T(2,128)} %bitcast.13, s32[2,8]{1,0:T(2,128)} %bitcast.14, s32[2,2,8]{2,1,0:T(2,128)} %bitcast.12, bf16[2,128,1024]{2,1,0:T(8,128)(2,1)} %bitcast.10), custom_call_target="tpu_custom_call" | custom-call | flops 100000000 | bytes 2129920 | tf_op jit(solution)/shard_map/pallas_call | solution.py:291
  3.4 0.0 copy-start.1
  3.4 0.0 copy-start.2
  3.4 0.0 copy-start.3
  3.4 10.5 %all-to-all-start = ((bf16[8,528,128]{2,1,0:T(8,128)(2,1)}), bf16[8,528,128]{2,1,0:T(8,128)(2,1)S(1)}, u32[]{:S(2)}, u32[]{:S(2)}) async-start(bf16[8,528,128]{2,1,0:T(8,128)(2,1)} %shard_map.95), calls=%async_computation | async-start | bytes 2162688 | tf_op jit(solution)/shard_map/all_to_all | solution.py:332
  13.9 0.0 copy-done
  13.9 0.7 collective-permute-start
  14.6 0.0 collective-permute-done.pair.old
  14.6 0.0 copy-done.1
  14.6 0.0 copy-done.2
  14.6 0.4 shard_map.96.tiles
  15.0 28.3 %all-to-all-done.got = bf16[8,528,128]{2,1,0:T(8,128)(2,1)S(1)} async-done(((bf16[8,528,128]{2,1,0:T(8,128)(2,1)}), bf16[8,528,128]{2,1,0:T(8,128)(2,1)S(1)}, u32[]{:S(2)}, u32[]{:S(2)}) %all-to-all-start) | async-done | bytes 1081376 | tf_op jit(solution)/shard_map/all_to_all | solution.py:332
  43.3 0.0 copy-done.3
  43.3 4.2 %shard_map.97 = (bf16[8,264,128]{2,1,0:T(8,128)(2,1)S(1)}, f32[16,256,256]{2,1,0:T(8,128)S(1)}, bf16[32,128,128]{2,1,0:T(8,128)(2,1)S(1)}, f32[16,8,128]{2,1,0:T...) custom-call(bf16[8,528,128]{2,1,0:T(8,128)(2,1)S(1)} %all-to-all-done.got, f32[256,256]{1,0:T(8,128)S(1)} %shard_map.96.tiles, ...), custom_call_target="tpu_custom_call" | custom-call | flops 1000000000 | bytes 6967296 | tf_op jit(solution)/shard_map/pallas_call | solution.py:291
  47.6 22.9 %all_to_all.20.got = bf16[8,264,128]{2,1,0:T(8,128)(2,1)S(1)} all-to-all(bf16[8,264,128]{2,1,0:T(8,128)(2,1)S(1)} %get-tuple-element.12), channel_id=1, replica_groups={{0,64,128,192,256,320,384,448},{8,72,136,200,264,328,392,456},{16,80,14..., dimensions={0} | all-to-all | bytes 1081344 | tf_op jit(solution)/shard_map/all_to_all | solution.py:332
  70.4 3.1 %shard_map.98 = (f32[16,40,128]{2,1,0:T(8,128)S(1)}, f32[8,128]{1,0:T(8,128)S(1)}) custom-call(bf16[8,264,128]{2,1,0:T(8,128)(2,1)S(1)} %all_to_all.20.got, bf16[256,128]{1,0:T(8,128)(2,1)S(1)} %collective-permute-done.pair.old, f32[16,256,256]{2,1,0:T(8,128)S(1)} %get-tuple-element.13.spec, bf16[32,128,128]{2,1,0:T(8,128)(2,1)S(1)} %get-tuple-element.14.moved, ...), custom_call_target="tpu_custom_call" | custom-call | flops 1000000000 | bytes 1380352 | tf_op jit(solution)/shard_map/pallas_call | solution.py:291
  73.6 16.5 %all_to_all.21.got = f32[16,40,128]{2,1,0:T(8,128)S(1)} all-to-all(f32[16,40,128]{2,1,0:T(8,128)S(1)} %get-tuple-element.18), channel_id=1, replica_groups={{1,65,129,193,257,321,385,449,7,71,135,199,263,327,391,455},{2,66,130,1..., dimensions={0} | all-to-all | bytes 655360 | tf_op jit(solution)/shard_map/all_to_all | solution.py:332
  90.1 0.1 shard_map.99
  90.1 28.7 %all_to_all.22 = bf16[64,40,128]{2,1,0:T(8,128)(2,1)S(1)} all-to-all(bf16[64,40,128]{2,1,0:T(8,128)(2,1)S(1)} %shard_map.99), channel_id=1, replica_groups=mesh['tm'=64,'plane'=8] {'tm'}, dimensions={0} | all-to-all | bytes 1310720 | tf_op jit(solution)/shard_map/all_to_all | solution.py:332
  118.9 1.5 %shard_map.100 = (bf16[16,8,16,128]{3,2,1,0:T(8,128)(2,1)}, f32[2,1,2,1,8]{4,3,2,1,0:T(1,128)}) custom-call(bf16[8,8,40,128]{3,2,1,0:T(8,128)(2,1)S(1)} %bitcast.9), custom_call_target="tpu_custom_call" | custom-call | flops 100000000 | bytes 1572992 | tf_op jit(solution)/shard_map/pallas_call | solution.py:291
  (1 shorter events, 0.0 us)
Async XLA Ops:
  0.6 13.3 %copy-start = (bf16[16,128,128]{2,1,0:T(8,128)(2,1)S(1)}, bf16[16,128,128]{2,1,0:T(8,128)(2,1)}, u32[]{:S(2)}) copy-start(bf16[16,128,128]{2,1,0:T(8,128)(2,1)} %param.12) | copy-start | bytes 1572868
  3.4 11.2 %copy-start.1 = (bf16[256,256]{1,0:T(8,128)(2,1)S(1)}, bf16[256,256]{1,0:T(8,128)(2,1)}, u32[]{:S(2)}) copy-start(bf16[256,256]{1,0:T(8,128)(2,1)} %constant.24.clone.left) | copy-start | bytes 393220
  3.4 11.2 %copy-start.2 = (bf16[128,256]{1,0:T(8,128)(2,1)S(1)}, bf16[128,256]{1,0:T(8,128)(2,1)}, u32[]{:S(2)}) copy-start(bf16[128,256]{1,0:T(8,128)(2,1)} %constant.23.clone.right) | copy-start | bytes 196612
  3.4 39.9 %copy-start.3 = (bf16[128,256]{1,0:T(8,128)(2,1)S(1)}, bf16[128,256]{1,0:T(8,128)(2,1)}, u32[]{:S(2)}) copy-start(bf16[128,256]{1,0:T(8,128)(2,1)} %constant.25.clone.rows) | copy-start | bytes 196612
  3.4 39.9 %all-to-all-start = ((bf16[8,528,128]{2,1,0:T(8,128)(2,1)}), bf16[8,528,128]{2,1,0:T(8,128)(2,1)S(1)}, u32[]{:S(2)}, u32[]{:S(2)}) async-start(bf16[8,528,128]{2,1,0:T(8,128)(2,1)} %shard_map.95), calls=%async_computation | async-start | bytes 2162688 | tf_op jit(solution)/shard_map/all_to_all | solution.py:332
  13.9 0.7 collective-permute-start

commit v9 on v6

--- a/solution.py
+++ b/solution.py
@@ -115,7 +115,7 @@
 
 
 def along_of(both, tiles, info, phase):
-    outs = []
+    parts = []
     for e in range(2):
         p_re, p_im = both[:N, e * N : (e + 1) * N], both[N:, e * N : (e + 1) * N]
         upper = info[e : e + 1, 0:1] > 0.5
@@ -126,13 +126,16 @@
         modulus = jnp.sqrt(c_re * c_re + c_im * c_im)
         level = jnp.sum(jnp.sum(modulus, 0, keepdims=True), 1, keepdims=True) * (1.0 / (N * N))
         scale = 1.0 / (modulus + 0.1 * level + 1e-06)
-        n_re = (c_re * scale).astype(BF16)
-        n_im = (c_im * scale).astype(BF16)
-        lhs = jnp.concatenate([phase[e : e + 1], phase[2 + e : 3 + e]], 0).astype(BF16)
-        s_re, s_im = dot(lhs, n_re), dot(lhs, n_im)
+        parts.append(((c_re * scale).astype(BF16), (c_im * scale).astype(BF16)))
+    lhs = phase[0:4].astype(BF16)
+    s_re = dot(lhs, jnp.concatenate([parts[0][0], parts[1][0]], 1))
+    s_im = dot(lhs, jnp.concatenate([parts[0][1], parts[1][1]], 1))
+    outs = []
+    for e in range(2):
+        at = slice(e * N, (e + 1) * N)
         outs.append(
-            phase[4 + e : 5 + e] * (s_re[0:1] - s_im[1:2])
-            - phase[6 + e : 7 + e] * (s_re[1:2] + s_im[0:1])
+            phase[4 + e : 5 + e] * (s_re[e : e + 1, at] - s_im[2 + e : 3 + e, at])
+            - phase[6 + e : 7 + e] * (s_re[2 + e : 3 + e, at] + s_im[e : e + 1, at])
         )
     return jnp.concatenate(outs, 0)
 

time: 118 us -> 117 us (level)
  no operation moved by 1% of the time
where the time goes in v9:
time: 117 us
  blocking collectives  64.9 us (55%)
  waiting for transfers between devices  28.3 us (24%)
  Pallas kernels  11.8 us (10%)
  starting transfers between devices  11.1 us (9%)
    all_to_all x3, blocking collectives, exchange(): lax.all_to_all(value, axis, split_axis=0, concat_axis=0, axis_index_group...  64.9 us
    all_to_all x1, waiting for transfers between devices, exchange(): lax.all_to_all(value, axis, split_axis=0, concat_axis=0, axis_index_group...  28.3 us
    pallas_call x6, Pallas kernels, call(): pl.pallas_call(kernel, out_shape=outs, in_specs=[pl.BlockSpec(memory_spac...  11.8 us
    all_to_all x1, starting transfers between devices, exchange(): lax.all_to_all(value, axis, split_axis=0, concat_axis=0, axis_index_group...  10.5 us
  transfers between devices with their start and end apart: 2, of which 1 were waited for; matrix products, arithmetic and copies ran while one was open for 0% of the time, Pallas kernels for 0%

profile of v9, /device:TPU:16, one launch (start us, length us, event | category | flops | bytes accessed | tf_op | source)
XLA Modules:
  0.0 117.0 jit_solution(6276782386499810041)
XLA Ops:
  0.6 0.0 copy-start
  0.6 2.7 %shard_map.95 = bf16[8,528,128]{2,1,0:T(8,128)(2,1)} custom-call(s32[2,2]{1,0:T(2,128)} %bitcast.13, s32[2,8]{1,0:T(2,128)} %bitcast.14, s32[2,2,8]{2,1,0:T(2,128)} %bitcast.12, bf16[2,128,1024]{2,1,0:T(8,128)(2,1)} %bitcast.10), custom_call_target="tpu_custom_call" | custom-call | flops 100000000 | bytes 2129920 | tf_op jit(solution)/shard_map/pallas_call | solution.py:298
  3.4 0.0 copy-start.1
  3.4 0.0 copy-start.2
  3.4 0.0 copy-start.3
  3.4 10.5 %all-to-all-start = ((bf16[8,528,128]{2,1,0:T(8,128)(2,1)}), bf16[8,528,128]{2,1,0:T(8,128)(2,1)S(1)}, u32[]{:S(2)}, u32[]{:S(2)}) async-start(bf16[8,528,128]{2,1,0:T(8,128)(2,1)} %shard_map.95), calls=%async_computation | async-start | bytes 2162688 | tf_op jit(solution)/shard_map/all_to_all | solution.py:339
  13.9 0.0 copy-done
  13.9 0.7 collective-permute-start
  14.6 0.0 collective-permute-done.pair.old
  14.6 0.0 copy-done.1
  14.6 0.0 copy-done.2
  14.6 0.4 shard_map.96.tiles
  15.0 28.3 %all-to-all-done.got = bf16[8,528,128]{2,1,0:T(8,128)(2,1)S(1)} async-done(((bf16[8,528,128]{2,1,0:T(8,128)(2,1)}), bf16[8,528,128]{2,1,0:T(8,128)(2,1)S(1)}, u32[]{:S(2)}, u32[]{:S(2)}) %all-to-all-start) | async-done | bytes 1081376 | tf_op jit(solution)/shard_map/all_to_all | solution.py:339
  43.3 0.0 copy-done.3
  43.3 4.0 %shard_map.97 = (bf16[8,264,128]{2,1,0:T(8,128)(2,1)S(1)}, f32[16,256,256]{2,1,0:T(8,128)S(1)}, bf16[32,128,128]{2,1,0:T(8,128)(2,1)S(1)}, f32[16,8,128]{2,1,0:T...) custom-call(bf16[8,528,128]{2,1,0:T(8,128)(2,1)S(1)} %all-to-all-done.got, f32[256,256]{1,0:T(8,128)S(1)} %shard_map.96.tiles, ...), custom_call_target="tpu_custom_call" | custom-call | flops 1000000000 | bytes 6967296 | tf_op jit(solution)/shard_map/pallas_call | solution.py:298
  47.4 22.9 %all_to_all.20.got = bf16[8,264,128]{2,1,0:T(8,128)(2,1)S(1)} all-to-all(bf16[8,264,128]{2,1,0:T(8,128)(2,1)S(1)} %get-tuple-element.12), channel_id=1, replica_groups={{0,64,128,192,256,320,384,448},{8,72,136,200,264,328,392,456},{16,80,14..., dimensions={0} | all-to-all | bytes 1081344 | tf_op jit(solution)/shard_map/all_to_all | solution.py:339
  70.3 3.1 %shard_map.98 = (bf16[16,40,128]{2,1,0:T(8,128)(2,1)S(1)}, f32[8,128]{1,0:T(8,128)S(1)}) custom-call(bf16[8,264,128]{2,1,0:T(8,128)(2,1)S(1)} %all_to_all.20.got, bf16[256,128]{1,0:T(8,128)(2,1)S(1)} %collective-permute-done.pair.old, f32[16,256,256]{2,1,0:T(8,128)S(1)} %get-tuple-element.13.spec, bf16[32,128,128]{2,1,0:T(8,128)(2,1)S(1)} %get-tuple-element.14.moved, ...), custom_call_target="tpu_custom_call" | custom-call | flops 1000000000 | bytes 1216512 | tf_op jit(solution)/shard_map/pallas_call | solution.py:298
  73.4 15.3 %all_to_all.21.got = bf16[16,40,128]{2,1,0:T(8,128)(2,1)S(1)} all-to-all(bf16[16,40,128]{2,1,0:T(8,128)(2,1)S(1)} %get-tuple-element.18), channel_id=1, replica_groups={{1,65,129,193,257,321,385,449,7,71,135,199,263,327,391,455},{2,66,130,1..., dimensions={0} | all-to-all | bytes 327680 | tf_op jit(solution)/shard_map/all_to_all | solution.py:339
  88.7 0.1 shard_map.99
  88.8 26.7 %all_to_all.22 = bf16[64,40,128]{2,1,0:T(8,128)(2,1)S(1)} all-to-all(bf16[64,40,128]{2,1,0:T(8,128)(2,1)S(1)} %shard_map.99), channel_id=1, replica_groups=mesh['tm'=64,'plane'=8] {'tm'}, dimensions={0} | all-to-all | bytes 1310720 | tf_op jit(solution)/shard_map/all_to_all | solution.py:339
  115.5 1.5 %shard_map.100 = (bf16[16,8,16,128]{3,2,1,0:T(8,128)(2,1)}, f32[2,1,2,1,8]{4,3,2,1,0:T(1,128)}) custom-call(bf16[8,8,40,128]{3,2,1,0:T(8,128)(2,1)S(1)} %bitcast.9), custom_call_target="tpu_custom_call" | custom-call | flops 100000000 | bytes 1572992 | tf_op jit(solution)/shard_map/pallas_call | solution.py:298
  (1 shorter events, 0.0 us)
Async XLA Ops:
  0.6 13.3 %copy-start = (bf16[16,128,128]{2,1,0:T(8,128)(2,1)S(1)}, bf16[16,128,128]{2,1,0:T(8,128)(2,1)}, u32[]{:S(2)}) copy-start(bf16[16,128,128]{2,1,0:T(8,128)(2,1)} %param.12) | copy-start | bytes 1572868
  3.4 11.2 %copy-start.1 = (bf16[256,256]{1,0:T(8,128)(2,1)S(1)}, bf16[256,256]{1,0:T(8,128)(2,1)}, u32[]{:S(2)}) copy-start(bf16[256,256]{1,0:T(8,128)(2,1)} %constant.24.clone.left) | copy-start | bytes 393220
  3.4 11.2 %copy-start.2 = (bf16[128,256]{1,0:T(8,128)(2,1)S(1)}, bf16[128,256]{1,0:T(8,128)(2,1)}, u32[]{:S(2)}) copy-start(bf16[128,256]{1,0:T(8,128)(2,1)} %constant.23.clone.right) | copy-start | bytes 196612
  3.4 39.9 %copy-start.3 = (bf16[128,256]{1,0:T(8,128)(2,1)S(1)}, bf16[128,256]{1,0:T(8,128)(2,1)}, u32[]{:S(2)}) copy-start(bf16[128,256]{1,0:T(8,128)(2,1)} %constant.25.clone.rows) | copy-start | bytes 196612
  3.4 39.9 %all-to-all-start = ((bf16[8,528,128]{2,1,0:T(8,128)(2,1)}), bf16[8,528,128]{2,1,0:T(8,128)(2,1)S(1)}, u32[]{:S(2)}, u32[]{:S(2)}) async-start(bf16[8,528,128]{2,1,0:T(8,128)(2,1)} %shard_map.95), calls=%async_computation | async-start | bytes 2162688 | tf_op jit(solution)/shard_map/all_to_all | solution.py:339
  13.9 0.7 collective-permute-start
